TPU v7x, 512 devices: a whole 4x8x8 slice. The times are simulated.
512 devices in a mesh: dp: 8 (over y_hi, core), seq: 64 (over y_lo, x, z).
Axes of the slice: x: 4, y: 8 (y_hi: 4, y_lo: 2; y = y_hi * 2 + y_lo), z: 8, core: 2. Of those that a mesh axis runs over, the one named last changes fastest.
Arguments:
- queries: bfloat16 [8, 8192, 512], P('dp', 'seq'), may hold values from -6 to 6
- keys: bfloat16 [8, 8192, 512], P('dp', 'seq'), may hold values from -6 to 6
- values: bfloat16 [8, 8192, 512], P('dp', 'seq'), may hold values from -12 to 12
- residual: bfloat16 [8, 8192, 1024], P('dp', 'seq'), may hold values from -3 to 3
- out_proj: bfloat16 [512, 1024], replicated, may hold values from -0.25 to 0.25
- conv_in: bfloat16 [1024, 2048], P(None, 'seq'), may hold values from -0.1875 to 0.1875
- conv_out: bfloat16 [1024, 1024], replicated, may hold values from -0.1875 to 0.1875
- depth_kernel: bfloat16 [31, 1024], replicated, may hold values from -1 to 1
- norm_gain: float32 [1024], replicated, may hold values from 0.25 to 1.75
- cotangent: bfloat16 [8, 8192, 1024], P('dp', 'seq'), may hold values from -6 to 6
Outputs:
- layer_out: bfloat16 [8, 8192, 1024], P('dp', 'seq')
- grad_mid: bfloat16 [8, 8192, 1024], P('dp', 'seq')
- grad_out_proj: float32 [512, 1024], P('seq')
- grad_kernel: float32 [31, 1024], replicated
All inputs are finite; a program needn't handle non-finite values.
Results may differ from a plain program's by a relative error of at most 0.015.
Values may be sent and summed in bfloat16 or wider, within the bound.
No kernel may reach another device: no remote copies, remote signals or barrier semaphores. Data moves between devices by JAX's collectives and lax.ppermute only.
A program may use at most 128 MiB of HBM per device.

v0:
```python
import math

import jax
import jax.numpy as jnp
from jax import lax
from jax.sharding import PartitionSpec as P

HEADS = 8
DH = 64
KW = 31


norm_epsilon = 1e-05


def padded_2(cells, sides, width):
    for axis, dim in sides:
        count = lax.axis_size(axis)
        ends = count - 1
        head = lax.slice_in_dim(cells, 0, width, axis=dim)
        tail = lax.slice_in_dim(cells, cells.shape[dim] - width, cells.shape[dim], axis=dim)
        cells = jnp.concatenate(
            [
                lax.ppermute(tail, axis, [(i, (i + 1) % count) for i in range(ends)]),
                cells,
                lax.ppermute(head, axis, [((i + 1) % count, i) for i in range(ends)]),
            ],
            axis=dim,
        )
    return cells


def attend_one(triple):
    query, key_rows, value_rows = triple
    length = query.shape[0]
    block = math.gcd(length, 512)
    query_blocks = query.reshape(length // block, block, query.shape[1])

    def one_block(query_block):
        scores = lax.dot_general(
            query_block, key_rows, (((1,), (1,)), ((), ())), preferred_element_type=jnp.float32
        ) * DH ** (-0.5)
        highest = jnp.max(scores, axis=1, keepdims=True)
        expo = jnp.exp(scores - highest)
        total = jnp.sum(expo, axis=1, keepdims=True)
        weights = expo.astype(jnp.bfloat16)
        mixed = jnp.dot(weights, value_rows, preferred_element_type=jnp.float32)
        return (mixed / total).astype(jnp.bfloat16)

    return lax.map(one_block, query_blocks).reshape(length, query.shape[1])


def attend_items(pieces):
    query_all, key_all, value_all = pieces
    return lax.map(attend_one, (query_all[0], key_all[0], value_all[0]))[None]


def layer_norm(mid):
    wide = mid.astype(jnp.float32)
    centered = wide - jnp.mean(wide, axis=-1, keepdims=True)
    rscale = lax.rsqrt(jnp.mean(centered * centered, axis=-1, keepdims=True) + norm_epsilon)
    return (centered * rscale, rscale)


def depth_forward(padded, kernel, rows):
    total = jnp.zeros((padded.shape[0], rows, padded.shape[2]), jnp.float32)
    for offset in range(KW):
        total = total + kernel[offset].astype(jnp.float32) * padded[
            :, offset : offset + rows
        ].astype(jnp.float32)
    return total


def depth_backward(padded, kernel, rows):
    total = jnp.zeros((padded.shape[0], rows, padded.shape[2]), jnp.float32)
    reach = (KW - 1) // 2
    for offset in range(KW):
        begin = 2 * reach - offset
        total = total + kernel[offset].astype(jnp.float32) * padded[:, begin : begin + rows].astype(
            jnp.float32
        )
    return total


def kernel_terms(padded, grad_conv, rows):
    terms = []
    for offset in range(KW):
        product = padded[:, offset : offset + rows].astype(jnp.float32) * grad_conv.astype(
            jnp.float32
        )
        terms.append(jnp.sum(product, axis=(0, 1)))
    return jnp.stack(terms, axis=0)


def body(
    queries, keys, values, residual, out_proj, conv_in, conv_out, depth_kernel, norm_gain, cotangent
):
    seq_count = lax.axis_size("seq")
    group = seq_count // HEADS
    batch, rows, width = queries.shape
    model = residual.shape[2]
    part = rows // group
    flat = batch * rows
    reach = (KW - 1) // 2
    query_send = (
        queries.reshape(batch, group, part, HEADS, DH)
        .transpose(3, 1, 0, 2, 4)
        .reshape(seq_count, batch, part, DH)
    )
    key_heads = keys.reshape(batch, rows, HEADS, DH).transpose(2, 0, 1, 3)
    value_heads = values.reshape(batch, rows, HEADS, DH).transpose(2, 0, 1, 3)
    key_send = jnp.broadcast_to(key_heads[:, None], (HEADS, group, batch, rows, DH)).reshape(
        seq_count, batch, rows, DH
    )
    value_send = jnp.broadcast_to(value_heads[:, None], (HEADS, group, batch, rows, DH)).reshape(
        seq_count, batch, rows, DH
    )
    attended_heads = attend_items(
        (
            lax.all_to_all(query_send, "seq", split_axis=0, concat_axis=2, tiled=True),
            lax.all_to_all(key_send, "seq", split_axis=0, concat_axis=2, tiled=True),
            lax.all_to_all(value_send, "seq", split_axis=0, concat_axis=2, tiled=True),
        )
    )
    returned = lax.all_to_all(
        attended_heads.reshape(1, batch, seq_count, part, DH),
        "seq",
        split_axis=2,
        concat_axis=0,
        tiled=True,
    )
    attended = (
        returned.reshape(HEADS, group, batch, part, DH)
        .transpose(2, 1, 3, 0, 4)
        .reshape(flat, width)
    )
    flat_resid = residual.reshape(flat, model).astype(jnp.float32)
    mid = (flat_resid + jnp.dot(attended, out_proj, preferred_element_type=jnp.float32)).astype(
        jnp.bfloat16
    )
    hat, rscale = layer_norm(mid)
    normed = (hat * norm_gain).astype(jnp.bfloat16)
    proj = jnp.dot(
        normed,
        lax.all_gather(conv_in, "seq", axis=1, tiled=True),
        preferred_element_type=jnp.float32,
    )
    value_half = proj[:, :model]
    gate_half = jax.nn.sigmoid(proj[:, model:])
    gated = (value_half * gate_half).astype(jnp.bfloat16).reshape(batch, rows, model)
    padded = padded_2(gated, (("seq", 1),), reach)
    conv = depth_forward(padded, depth_kernel, rows)
    act = (conv * jax.nn.sigmoid(conv)).astype(jnp.bfloat16).reshape(flat, model)
    layer_out = (
        mid.astype(jnp.float32) + jnp.dot(act, conv_out, preferred_element_type=jnp.float32)
    ).astype(jnp.bfloat16)
    flat_cot = cotangent.reshape(flat, model)
    grad_act = lax.dot_general(
        flat_cot, conv_out, (((1,), (1,)), ((), ())), preferred_element_type=jnp.float32
    )
    sig_conv = jax.nn.sigmoid(conv).reshape(flat, model)
    conv_flat = conv.reshape(flat, model)
    grad_conv = (
        (grad_act * sig_conv * (1.0 + conv_flat * (1.0 - sig_conv)))
        .astype(jnp.bfloat16)
        .reshape(batch, rows, model)
    )
    grad_padded = padded_2(grad_conv, (("seq", 1),), reach)
    grad_gated = depth_backward(grad_padded, depth_kernel, rows).reshape(flat, model)
    grad_kernel = lax.psum(kernel_terms(padded, grad_conv, rows), ("dp", "seq"))
    grad_proj = jnp.concatenate(
        [grad_gated * gate_half, grad_gated * value_half * gate_half * (1.0 - gate_half)], axis=1
    ).astype(jnp.bfloat16)
    grad_normed = lax.dot_general(
        grad_proj,
        lax.all_gather(conv_in, "seq", axis=1, tiled=True),
        (((1,), (1,)), ((), ())),
        preferred_element_type=jnp.float32,
    )
    scaled = grad_normed * norm_gain
    inner = (
        scaled
        - jnp.mean(scaled, axis=1, keepdims=True)
        - hat * jnp.mean(scaled * hat, axis=1, keepdims=True)
    )
    grad_mid = (flat_cot.astype(jnp.float32) + rscale * inner).astype(jnp.bfloat16)
    partial_rows = lax.psum_scatter(
        lax.dot_general(
            attended, grad_mid, (((0,), (0,)), ((), ())), preferred_element_type=jnp.float32
        ),
        "seq",
        scatter_dimension=0,
        tiled=True,
    )
    grad_out_proj = lax.psum(partial_rows.astype(jnp.bfloat16), "dp").astype(jnp.float32)
    return (
        layer_out.reshape(batch, rows, model),
        grad_mid.reshape(batch, rows, model),
        grad_out_proj,
        grad_kernel,
    )


def solution(mesh):
    return jax.shard_map(
        body,
        mesh=mesh,
        in_specs=(
            P("dp", "seq", None),
            P("dp", "seq", None),
            P("dp", "seq", None),
            P("dp", "seq", None),
            P(),
            P(None, "seq"),
            P(),
            P(),
            P(),
            P("dp", "seq", None),
        ),
        out_specs=(P("dp", "seq", None), P("dp", "seq", None), P("seq", None), P()),
        check_vma=False,
    )
```

profile of v0, /device:TPU:1, one launch (start us, length us, event | category | flops | bytes accessed | tf_op | source)
XLA Modules:
  0.0 1025.3 jit_solution(12149460593854754452)
XLA Ops:
  9.4 15.3 %all-to-all-start = ((bf16[64,2,512]{2,1,0:T(2,128)(2,1)}), bf16[64,2,512]{2,1,0:T(2,128)(2,1)S(1)}, u32[]{:S(2)}, u32[]{:S(2)}) async-start(bf16[64,2,512]{2,1,0:T(2,128)(2,1)} %reshape.454), calls=%async_computation | async-start | bytes 262144 | tf_op jit(solution)/shard_map/all_to_all | solution.py:120
  25.7 8.6 all-to-all-done
  35.6 4.8 all-to-all-start.1
  40.5 28.2 %all-to-all-done.1 = bf16[64,1,128,64]{2,3,1,0:T(8,128)(2,1)S(1)} async-done(((bf16[64,1,128,64]{2,3,1,0:T(8,128)(2,1)}), bf16[64,1,128,64]{2,3,1,0:T(8,128)(2,1)S(1)}, u32[]{:S(2)}, u32[]{:S(2)}) %all-to-all-start.1) | async-done | bytes 1048608 | tf_op jit(solution)/shard_map/all_to_all | solution.py:121
  70.0 7.0 all-to-all-start.2
  78.0 1.8 copy.40
  79.8 26.2 %all-to-all-done.2 = bf16[64,1,128,64]{2,3,1,0:T(8,128)(2,1)} async-done(((bf16[64,1,128,64]{2,3,1,0:T(8,128)(2,1)}), bf16[64,1,128,64]{2,3,1,0:T(8,128)(2,1)}, u32[]{:S(2)}, u32[]{:S(2)}) %all-to-all-start.2) | async-done | bytes 1048608 | tf_op jit(solution)/shard_map/all_to_all | solution.py:122
  106.0 2.7 copy.41
  108.7 52.2 %while.17 = (s32[]{:T(128)}, bf16[2,512,64]{1,2,0:T(8,128)(2,1)S(1)}, bf16[2,512,64]{2,1,0:T(8,128)(2,1)S(1)}, bf16[8192,64]{1,0:T(8,128)(2,1)}, bf16[8192,64]{1,0:T(8,128)(2,1)}, /*index=5*/s32[]{:T(128)}) while((s32[]{:T(128)}, bf16[2,512,64]{1,2,0:T(8,128)(2,1)S(1)}, bf16[2,512,64]{2,1,0:T(8,128)(2,1)S(1)}, bf16[8192,64]{1,0:T(8,128)(2,1)}, ...), condition=%wide.region_3.4_spmd, body=%wide.region_0.3_spmd.sunk | while | flops 1107360768 | bytes 57878632 | solution.py:50
  108.7 9.7 multiply_reduce_fusion.4
  118.4 8.8 fusion.236
  127.2 7.6 fusion.237
  134.8 9.6 multiply_reduce_fusion.4
  144.5 8.8 fusion.236
  153.3 7.6 fusion.237
  161.9 7.4 all-to-all-start.3
  169.6 9.4 all-to-all-done.3
  182.3 161.4 %all-gather.2.cloned.1.call-done = bf16[1024,2048]{0,1:T(8,128)(2,1)} async-done(((bf16[1024,32]{0,1:T(8,128)(2,1)}), bf16[1024,2048]{0,1:T(8,128)(2,1)}) %all-gather.2.cloned.1.call-update) | async-done | bytes 4194320 | tf_op jit(solution)/shard_map/all_gather | solution.py:145
  343.7 3.9 fusion.147
  350.7 3.6 collective-permute-done.1
  354.9 2.5 fusion.87
  358.4 1.9 fusion.101
  361.8 4.0 collective-permute-start.3
  367.0 2.6 fusion.142
  373.8 2.6 fusion.116
  376.5 3.6 fusion.117
  380.0 3.4 fusion.102
  383.5 2.7 stack.127
  386.2 2.4 fusion.26
  388.6 313.2 %reduce-scatter.2.cloned.1.call-done = f32[8,1024]{1,0:T(8,128)} async-done(((f32[512,1024]{1,0:T(8,128)}), f32[8,1024]{1,0:T(8,128)}) %reduce-scatter.2.cloned.1.call-update) | async-done | bytes 32784 | tf_op jit(solution)/shard_map/reduce_scatter | solution.py:187
  702.5 74.3 %psum.14 = bf16[8,1024]{1,0:T(8,128)(2,1)S(1)} all-reduce(bf16[8,1024]{1,0:T(8,128)(2,1)S(1)} %convert_element_type.775), channel_id=1, replica_groups=mesh['dp'=8,'seq'=64] {'dp'}, use_global_device_ids=true, to_apply=%region_9.10 | all-reduce | flops 8192 | bytes 32768 | tf_op jit(solution)/shard_map/psum | solution.py:195
  777.4 239.8 %all-reduce.2.cloned.1.call-done = f32[31,1024]{1,0:T(8,128)} async-done(((f32[31,1024]{1,0:T(8,128)}), f32[31,1024]{1,0:T(8,128)}) %all-reduce.2.cloned.1.call-update) | async-done | bytes 126992 | tf_op jit(solution)/shard_map/psum | solution.py:170
  (162 shorter events, 25.1 us)
Async XLA Ops:
  7.2 351.1 %copy-start = (bf16[1024,1024]{1,0:T(8,128)(2,1)S(1)}, bf16[1024,1024]{1,0:T(8,128)(2,1)}, u32[]{:S(2)}) copy-start(bf16[1024,1024]{1,0:T(8,128)(2,1)} %param.18) | copy-start | bytes 6291460
  9.4 25.0 %all-to-all-start = ((bf16[64,2,512]{2,1,0:T(2,128)(2,1)}), bf16[64,2,512]{2,1,0:T(2,128)(2,1)S(1)}, u32[]{:S(2)}, u32[]{:S(2)}) async-start(bf16[64,2,512]{2,1,0:T(2,128)(2,1)} %reshape.454), calls=%async_computation | async-start | bytes 262144 | tf_op jit(solution)/shard_map/all_to_all | solution.py:120
  35.6 33.2 %all-to-all-start.1 = ((bf16[64,1,128,64]{2,3,1,0:T(8,128)(2,1)}), bf16[64,1,128,64]{2,3,1,0:T(8,128)(2,1)S(1)}, u32[]{:S(2)}, u32[]{:S(2)}) async-start(bf16[64,1,128,64]{2,3,1,0:T(8,128)(2,1)} %bitcast.326), calls=%async_computation.1 | async-start | bytes 2097152 | tf_op jit(solution)/shard_map/all_to_all | solution.py:121
  70.0 36.0 %all-to-all-start.2 = ((bf16[64,1,128,64]{2,3,1,0:T(8,128)(2,1)}), bf16[64,1,128,64]{2,3,1,0:T(8,128)(2,1)}, u32[]{:S(2)}, u32[]{:S(2)}) async-start(bf16[64,1,128,64]{2,3,1,0:T(8,128)(2,1)} %bitcast.325), calls=%async_computation.2 | async-start | bytes 2097152 | tf_op jit(solution)/shard_map/all_to_all | solution.py:122
  77.0 266.7 %all-gather.2.cloned.1.call-start = ((), (), s32[]{:S(2)}) async-start(), calls=%async_computation.5 | async-start | bytes 4259840 | tf_op jit(solution)/shard_map/all_gather | solution.py:145
  108.7 70.9 %copy-start.9 = (bf16[1,128,1024]{2,1,0:T(8,128)(2,1)S(1)}, bf16[1,128,1024]{2,1,0:T(8,128)(2,1)}, u32[]{:S(2)}) copy-start(bf16[1,128,1024]{2,1,0:T(8,128)(2,1)} %param.15) | copy-start | bytes 786436
  160.9 182.8 %copy-start.46 = (f32[1024]{0:T(1024)S(1)}, f32[1024]{0:T(1024)}, u32[]{:S(2)}) copy-start(f32[1024]{0:T(1024)} %param.20) | copy-start | bytes 12292
  161.9 17.1 %all-to-all-start.3 = ((bf16[64,2,512]{2,1,0:T(2,128)(2,1)}), bf16[64,2,512]{2,1,0:T(2,128)(2,1)S(1)}, u32[]{:S(2)}, u32[]{:S(2)}) async-start(bf16[64,2,512]{2,1,0:T(2,128)(2,1)} %reshape.456), calls=%async_computation.3 | async-start | bytes 262144 | tf_op jit(solution)/shard_map/all_to_all | solution.py:125
  169.4 532.4 %reduce-scatter.2.cloned.1.call-start = ((), (), s32[]{:S(2)}) async-start(), calls=%async_computation.6 | async-start | bytes 2129920 | tf_op jit(solution)/shard_map/reduce_scatter | solution.py:187
  169.5 184.8 %copy-start.16 = (f32[1,1024]{1,0:T(1,128)}, f32[1,1024]{1,0:T(1,128)S(1)}, u32[]{:S(2)}) copy-start(f32[1,1024]{1,0:T(1,128)S(1)} %get-tuple-element.106) | copy-start | bytes 12292
  169.5 184.8 %copy-start.18 = (f32[1,1024]{1,0:T(1,128)}, f32[1,1024]{1,0:T(1,128)S(1)}, u32[]{:S(2)}) copy-start(f32[1,1024]{1,0:T(1,128)S(1)} %get-tuple-element.107) | copy-start | bytes 12292
  169.5 184.8 %copy-start.20 = (f32[1,1024]{1,0:T(1,128)}, f32[1,1024]{1,0:T(1,128)S(1)}, u32[]{:S(2)}) copy-start(f32[1,1024]{1,0:T(1,128)S(1)} %get-tuple-element.108) | copy-start | bytes 12292
  169.5 184.8 %copy-start.22 = (f32[1,1024]{1,0:T(1,128)}, f32[1,1024]{1,0:T(1,128)S(1)}, u32[]{:S(2)}) copy-start(f32[1,1024]{1,0:T(1,128)S(1)} %get-tuple-element.109) | copy-start | bytes 12292
  169.5 184.8 %copy-start.24 = (f32[1,1024]{1,0:T(1,128)}, f32[1,1024]{1,0:T(1,128)S(1)}, u32[]{:S(2)}) copy-start(f32[1,1024]{1,0:T(1,128)S(1)} %get-tuple-element.110) | copy-start | bytes 12292
  169.5 184.8 %copy-start.26 = (f32[1,1024]{1,0:T(1,128)}, f32[1,1024]{1,0:T(1,128)S(1)}, u32[]{:S(2)}) copy-start(f32[1,1024]{1,0:T(1,128)S(1)} %get-tuple-element.111) | copy-start | bytes 12292
  169.6 184.8 %copy-start.28 = (f32[1,1024]{1,0:T(1,128)}, f32[1,1024]{1,0:T(1,128)S(1)}, u32[]{:S(2)}) copy-start(f32[1,1024]{1,0:T(1,128)S(1)} %get-tuple-element.112) | copy-start | bytes 12292
  169.6 184.8 %copy-start.30 = (f32[1,1024]{1,0:T(1,128)}, f32[1,1024]{1,0:T(1,128)S(1)}, u32[]{:S(2)}) copy-start(f32[1,1024]{1,0:T(1,128)S(1)} %get-tuple-element.113) | copy-start | bytes 12292
  169.6 184.8 %copy-start.32 = (f32[1,1024]{1,0:T(1,128)}, f32[1,1024]{1,0:T(1,128)S(1)}, u32[]{:S(2)}) copy-start(f32[1,1024]{1,0:T(1,128)S(1)} %get-tuple-element.114) | copy-start | bytes 12292
  169.6 184.8 %copy-start.34 = (f32[1,1024]{1,0:T(1,128)}, f32[1,1024]{1,0:T(1,128)S(1)}, u32[]{:S(2)}) copy-start(f32[1,1024]{1,0:T(1,128)S(1)} %get-tuple-element.115) | copy-start | bytes 12292
  169.6 184.8 %copy-start.36 = (f32[1,1024]{1,0:T(1,128)}, f32[1,1024]{1,0:T(1,128)S(1)}, u32[]{:S(2)}) copy-start(f32[1,1024]{1,0:T(1,128)S(1)} %get-tuple-element.116) | copy-start | bytes 12292
  169.6 184.8 %copy-start.38 = (f32[1,1024]{1,0:T(1,128)}, f32[1,1024]{1,0:T(1,128)S(1)}, u32[]{:S(2)}) copy-start(f32[1,1024]{1,0:T(1,128)S(1)} %get-tuple-element.117) | copy-start | bytes 12292
  169.6 184.8 %copy-start.40 = (f32[1,1024]{1,0:T(1,128)}, f32[1,1024]{1,0:T(1,128)S(1)}, u32[]{:S(2)}) copy-start(f32[1,1024]{1,0:T(1,128)S(1)} %get-tuple-element.118) | copy-start | bytes 12292
  169.6 184.8 %copy-start.42 = (f32[1,1024]{1,0:T(1,128)}, f32[1,1024]{1,0:T(1,128)S(1)}, u32[]{:S(2)}) copy-start(f32[1,1024]{1,0:T(1,128)S(1)} %get-tuple-element.119) | copy-start | bytes 12292
  169.6 184.8 %copy-start.44 = (f32[1,1024]{1,0:T(1,128)}, f32[1,1024]{1,0:T(1,128)S(1)}, u32[]{:S(2)}) copy-start(f32[1,1024]{1,0:T(1,128)S(1)} %get-tuple-element.120) | copy-start | bytes 12292
  181.3 169.4 %copy-start.12 = (bf16[31,1024]{1,0:T(8,128)(2,1)S(1)}, bf16[31,1024]{1,0:T(8,128)(2,1)}, u32[]{:S(2)}) copy-start(bf16[31,1024]{1,0:T(8,128)(2,1)} %param.19) | copy-start | bytes 190468
  181.3 167.8 %copy-start.48 = (f32[128]{0:T(128)}, f32[128]{0:T(128)S(1)}, u32[]{:S(2)}) copy-start(f32[128]{0:T(128)S(1)} %broadcast_multiply_fusion.2) | copy-start | bytes 1540
  182.3 166.9 %copy-start.50 = (f32[128]{0:T(128)}, f32[128]{0:T(128)S(1)}, u32[]{:S(2)}) copy-start(f32[128]{0:T(128)S(1)} %add_rsqrt_fusion) | copy-start | bytes 1540
  347.8 2.9 collective-permute-start
  349.1 5.2 collective-permute-start.1
  360.4 5.4 collective-permute-start.2
  361.8 5.0 collective-permute-start.3
  373.6 643.5 %all-reduce.2.cloned.1.call-start = ((), (), s32[]{:S(2)}) async-start(), calls=%async_computation.7 | async-start | bytes 262144 | tf_op jit(solution)/shard_map/psum | solution.py:170
  (38 other events, 429.3 us)
Sparse Core Ops, SparseCore 0:
  79.9 263.7 all-gather.1
  373.7 327.9 reduce-scatter.1
  707.3 309.8 all-reduce.1
where the time goes:
time: 1030 us
  waiting for transfers between devices  792 us (77%)
  blocking collectives  74.3 us (7%)
  matrix products  47.1 us (5%)
  starting transfers between devices  43.1 us (4%)
  other arithmetic  34.8 us (3%)
  local copies, waits for them, and re-layouts  19.4 us (2%)
  between operations  14.7 us (1%)
    reduce_scatter x1, waiting for transfers between devices, body(): lax.psum_scatter(lax.dot_general(attended, grad_mid, (((0,), (0,)), ((),...  313 us
    psum x1, waiting for transfers between devices, body(): grad_kernel = lax.psum(kernel_terms(padded, grad_conv, rows), ('dp', 'seq'))  240 us
    all_gather x1, waiting for transfers between devices, body(): lax.all_gather(conv_in, 'seq', axis=1, tiled=True)  161 us
    psum x1, blocking collectives, body(): lax.psum(partial_rows.astype(jnp.bfloat16), 'dp').astype(jnp.float32)  74.3 us
    all_to_all x1, waiting for transfers between devices, body(): lax.all_to_all(key_send, 'seq', split_axis=0, concat_axis=2, tiled=True)  28.2 us
    all_to_all x1, waiting for transfers between devices, body(): lax.all_to_all(value_send, 'seq', split_axis=0, concat_axis=2, tiled=True)  26.2 us
  transfers between devices with their start and end apart: 11, of which 9 were waited for; matrix products, arithmetic and copies ran while one was open for 8% of the time, Pallas kernels for 0%

commit v1 on v0

v1 whole, which is shorter than its diff:
```python
import math

import jax
import jax.numpy as jnp
from jax import lax
from jax.experimental import pallas as pl
from jax.experimental.pallas import tpu as pltpu
from jax.sharding import Mesh, PartitionSpec as P

HEADS = 8
DH = 64
KW = 31
REACH = (KW - 1) // 2
norm_epsilon = 1e-05

F32 = jnp.float32
BF16 = jnp.bfloat16

YX = ("yl", "x")
SEQ = ("yl", "x", "z")
NT = (((1,), (1,)), ((), ()))


def pack_kernel(q_ref, k_ref, v_ref, o_ref):
    for pair in range(HEADS // 2):
        cols = pl.ds(pair * 128, 128)
        q_t = q_ref[:, cols].astype(F32).T.astype(BF16)
        v_t = v_ref[:, cols].astype(F32).T.astype(BF16)
        upper = k_ref[0:64, cols].astype(F32)
        lower = k_ref[64:128, cols].astype(F32)
        lane = lax.broadcasted_iota(jnp.int32, upper.shape, 1)
        first = jnp.where(lane < 64, upper, pltpu.roll(lower, 64, 1)).astype(BF16)
        second = jnp.where(lane < 64, pltpu.roll(upper, 64, 1), lower).astype(BF16)
        for half, packed in ((0, first), (1, second)):
            head = 2 * pair + half
            o_ref[head, 0] = q_t[half * 64 : half * 64 + 64]
            o_ref[head, 1] = packed
            o_ref[head, 2] = v_t[half * 64 : half * 64 + 64]


def pack(q, k, v):
    return pl.pallas_call(
        pack_kernel,
        out_shape=jax.ShapeDtypeStruct((HEADS, 3, 64, 128), BF16),
    )(q, k, v)


SCALE = DH ** (-0.5) * math.log2(math.e)
QB = 256


def attend_kernel(q_ref, kv_ref, o_ref, r_lo, r_hi, top, acc):
    step = pl.program_id(0)
    count = q_ref.shape[0]
    width = count * 128

    @pl.when(step == 0)
    def _():
        for i in range(count):
            scaled = q_ref[i].astype(F32) * SCALE
            high = scaled.astype(BF16)
            low = (scaled - high.astype(F32)).astype(BF16)
            none = jnp.zeros_like(high)
            cols = pl.ds(i * 128, 128)
            r_lo[:, cols] = jnp.concatenate([high, none, low, none], axis=0)
            r_hi[:, cols] = jnp.concatenate([none, high, none, low], axis=0)
        top[...] = jnp.full(top.shape, -jnp.inf, F32)
        acc[...] = jnp.zeros(acc.shape, F32)

    sources = kv_ref.shape[0]
    packed = kv_ref[:, 0].reshape(sources * 64, 128)
    keys = jnp.concatenate([packed, packed], axis=1)
    values = jnp.concatenate([kv_ref[s, 1] for s in range(sources)], axis=1)
    values = jnp.concatenate([values, jnp.ones((16, sources * 128), BF16)], axis=0)
    for block in range(width // QB):
        cols = pl.ds(block * QB, QB)
        s_lo = jnp.dot(keys, r_lo[:, cols], preferred_element_type=F32)
        s_hi = jnp.dot(keys, r_hi[:, cols], preferred_element_type=F32)
        before = top[:, cols]
        highest = jnp.maximum(
            before, jnp.max(jnp.maximum(s_lo, s_hi), axis=0, keepdims=True)
        )
        top[:, cols] = highest
        p_lo = jnp.exp2(s_lo - highest).astype(BF16)
        p_hi = jnp.exp2(s_hi - highest).astype(BF16)
        pieces = []
        for s in range(sources):
            pieces.append(p_lo[s * 64 : s * 64 + 64])
            pieces.append(p_hi[s * 64 : s * 64 + 64])
        weights = jnp.concatenate(pieces, axis=0)
        mixed = jnp.dot(values, weights, preferred_element_type=F32)
        acc[:, cols] = acc[:, cols] * jnp.exp2(before - highest) + mixed

    @pl.when(step == pl.num_programs(0) - 1)
    def _():
        done = (acc[0:64] / acc[64:65]).astype(BF16)
        for i in range(count):
            o_ref[i] = done[:, i * 128 : i * 128 + 128]


def attend(q_t, kv):
    count = q_t.shape[0]
    sources = kv.shape[0]
    chunk = 8
    return pl.pallas_call(
        attend_kernel,
        grid=(sources // chunk,),
        in_specs=[
            pl.BlockSpec((count, 64, 128), lambda i: (0, 0, 0)),
            pl.BlockSpec((chunk, 2, 64, 128), lambda i: (i, 0, 0, 0)),
        ],
        out_specs=pl.BlockSpec((count, 64, 128), lambda i: (0, 0, 0)),
        out_shape=jax.ShapeDtypeStruct((count, 64, 128), BF16),
        scratch_shapes=[
            pltpu.VMEM((256, count * 128), BF16),
            pltpu.VMEM((256, count * 128), BF16),
            pltpu.VMEM((1, count * 128), F32),
            pltpu.VMEM((80, count * 128), F32),
        ],
        compiler_params=pltpu.CompilerParams(vmem_limit_bytes=56 * 1024 * 1024),
    )(q_t, kv)


def swap(array, axes):
    return lax.all_to_all(array, axes, split_axis=0, concat_axis=0, tiled=True)


def spread(array, axes, count):
    return swap(jnp.broadcast_to(array[None], (count,) + array.shape), axes)


def neighbours(rows, width):
    count = 64
    head = rows[:width]
    tail = rows[rows.shape[0] - width :]
    before = lax.ppermute(tail, SEQ, [(i, i + 1) for i in range(count - 1)])
    after = lax.ppermute(head, SEQ, [(i + 1, i) for i in range(count - 1)])
    return jnp.concatenate([before, rows, after], axis=0)


def layer_norm(mid):
    wide = mid.astype(F32)
    centered = wide - jnp.mean(wide, axis=-1, keepdims=True)
    rscale = lax.rsqrt(jnp.mean(centered * centered, axis=-1, keepdims=True) + norm_epsilon)
    return centered * rscale, rscale


def depth_forward(padded, kernel, rows):
    total = jnp.zeros((rows, padded.shape[1]), F32)
    for offset in range(KW):
        total = total + kernel[offset].astype(F32) * padded[offset : offset + rows].astype(F32)
    return total


def depth_backward(padded, kernel, rows):
    total = jnp.zeros((rows, padded.shape[1]), F32)
    for offset in range(KW):
        begin = 2 * REACH - offset
        total = total + kernel[offset].astype(F32) * padded[begin : begin + rows].astype(F32)
    return total


def kernel_terms(padded, grad_conv, rows):
    wide = grad_conv.astype(F32)
    terms = []
    for offset in range(KW):
        terms.append(jnp.sum(padded[offset : offset + rows].astype(F32) * wide, axis=0))
    terms.append(jnp.zeros_like(terms[0]))
    return jnp.stack(terms, axis=0)


def body(
    queries, keys, values, residual, out_proj, conv_in, conv_out, depth_kernel, norm_gain, cotangent
):
    rows = queries.shape[1]
    model = residual.shape[2]
    core = lax.axis_index("core")

    turned = conv_in.T
    share = lax.dynamic_slice_in_dim(turned, core * (model // 2), model // 2, axis=1)
    share = lax.all_gather(share, YX, axis=0, tiled=False)
    share = lax.all_gather(share, "z", axis=0, tiled=False)
    both = lax.all_gather(share, "core", axis=0, tiled=False)
    halves = [
        both[c].transpose(1, 0, 2, 3).reshape(2 * model, model // 2) for c in range(2)
    ]

    cot = cotangent[0]
    cot_wide = neighbours(cot, REACH)
    grad_act = lax.dot_general(cot_wide, conv_out, NT, preferred_element_type=F32)

    sent = pack(queries[0], keys[0], values[0])
    got = swap(sent, "z")
    kv = spread(got[:, 1:], YX, 8).reshape(64, 2, 64, 128)
    attended_t = swap(attend(got[:, 0], kv), "z").reshape(HEADS * DH, rows)

    flat_resid = residual[0].astype(F32)
    mid = (
        flat_resid
        + lax.dot_general(
            attended_t, out_proj, (((0,), (0,)), ((), ())), preferred_element_type=F32
        )
    ).astype(BF16)
    hat, rscale = layer_norm(mid)
    normed = (hat * norm_gain).astype(BF16)
    proj = lax.dot_general(
        normed[:, : model // 2], halves[0], NT, preferred_element_type=F32
    ) + lax.dot_general(normed[:, model // 2 :], halves[1], NT, preferred_element_type=F32)
    value_half = proj[:, :model]
    gate_half = jax.nn.sigmoid(proj[:, model:])
    gated = (value_half * gate_half).astype(BF16)
    padded = neighbours(gated, 2 * REACH)
    conv = depth_forward(padded, depth_kernel, rows + 2 * REACH)
    sig_conv = jax.nn.sigmoid(conv)
    act = (conv * sig_conv)[REACH : REACH + rows].astype(BF16)
    layer_out = (mid.astype(F32) + jnp.dot(act, conv_out, preferred_element_type=F32)).astype(BF16)
    grad_padded = (grad_act * sig_conv * (1.0 + conv * (1.0 - sig_conv))).astype(BF16)
    grad_gated = depth_backward(grad_padded, depth_kernel, rows)
    grad_kernel = kernel_terms(
        padded[REACH : REACH + rows + 2 * REACH], grad_padded[REACH : REACH + rows], rows
    )
    grad_proj = jnp.concatenate(
        [grad_gated * gate_half, grad_gated * value_half * gate_half * (1.0 - gate_half)], axis=1
    ).astype(BF16)
    grad_normed = jnp.concatenate(
        [jnp.dot(grad_proj, half, preferred_element_type=F32) for half in halves], axis=1
    )
    scaled = grad_normed * norm_gain
    inner = (
        scaled
        - jnp.mean(scaled, axis=1, keepdims=True)
        - hat * jnp.mean(scaled * hat, axis=1, keepdims=True)
    )
    grad_mid = (cot.astype(F32) + rscale * inner).astype(BF16)
    partial = jnp.dot(attended_t, grad_mid, preferred_element_type=F32)

    by_core = partial.reshape(8, 8, 2, 4, model).transpose(2, 0, 1, 3, 4).reshape(2, 256, model)
    both_sums = jnp.concatenate([by_core, grad_kernel.reshape(2, 16, model)], axis=1)
    sums = jnp.sum(swap(both_sums.astype(BF16), "core").astype(F32), axis=0)

    def joined(first, second, count):
        second = jnp.broadcast_to(second[None], (count,) + second.shape)
        return jnp.concatenate([first, second], axis=1)

    sums = joined(sums[:256].reshape(8, 32, model), sums[256:], 8)
    sums = jnp.sum(swap(sums.astype(BF16), YX).astype(F32), axis=0)
    sums = joined(sums[:32].reshape(8, 4, model), sums[32:], 8)
    sums = jnp.sum(swap(sums.astype(BF16), "z").astype(F32), axis=0)
    sums = jnp.sum(spread(sums, "yh", 4), axis=0)
    sums = spread(sums, "core", 2)
    grad_out_proj = sums[:, :4].reshape(8, model)
    grad_kernel = sums[:, 4:].reshape(32, model)[:KW]
    return layer_out[None], grad_mid[None], grad_out_proj, grad_kernel


def solution(mesh):
    split = Mesh(mesh.devices.reshape(4, 2, 2, 4, 8), ("yh", "core", "yl", "x", "z"))
    rows = P(("yh", "core"), SEQ, None)
    return jax.shard_map(
        body,
        mesh=split,
        in_specs=(rows, rows, rows, rows, P(), P(None, SEQ), P(), P(), P(), rows),
        out_specs=(rows, rows, P(SEQ, None), P()),
        check_vma=False,
    )
```

time: 1030 us -> 233 us (0.23)
  waiting for transfers between devices: 792 us -> 37.6 us
  matrix products: 47.1 us -> 8.72 us
  blocking collectives: 74.3 us -> 102 us
  Pallas kernels: 0 us -> 23.3 us
  other arithmetic: 34.8 us -> 13 us
  starting transfers between devices: 43.1 us -> 21.8 us
    reduce_scatter x1 -> x0, waiting for transfers between devices: 313 us -> none  [body(): lax.psum_scatter(lax.dot_general(attended, grad_mid, (((0,), (0,)), ((),...]
    psum x1 -> x0, waiting for transfers between devices: 240 us -> none  [body(): grad_kernel = lax.psum(kernel_terms(padded, grad_conv, rows), ('dp', 'seq'))]
    all_gather x1 -> x2, waiting for transfers between devices: 161 us -> 21 us  [the longest x1 21 us: body(): share = lax.all_gather(share, 'z', axis=0, tiled=False)]
    all_to_all x0 -> x5, blocking collectives: none -> 76.8 us  [swap(): return lax.all_to_all(array, axes, split_axis=0, concat_axis=0, tiled=True)]
    psum x1 -> x0, blocking collectives: 74.3 us -> none  [body(): lax.psum(partial_rows.astype(jnp.bfloat16), 'dp').astype(jnp.float32)]
    all_to_all x4 -> x3, waiting for transfers between devices: 72.3 us -> 13.1 us  [swap(): return lax.all_to_all(array, axes, split_axis=0, concat_axis=0, tiled=True)]
    dot_general x10 -> x8, matrix products: 47.1 us -> 8.72 us  [the longest x1 2.39 us: body(): jnp.dot(act, conv_out, preferred_element_type=F32)]
    all_gather x0 -> x1, blocking collectives: none -> 25.5 us  [body(): share = lax.all_gather(share, YX, axis=0, tiled=False)]
  transfers between devices with their start and end apart: 11 -> 9, of which waited for: 9 -> 5; matrix products, arithmetic and copies ran while one was open for 8% -> 7% of each run, Pallas kernels for 0% -> 10%
where the time goes in v1:
time: 233 us; the launch traced here: 232 us
  blocking collectives  102 us (44%)
  waiting for transfers between devices  37.6 us (16%)
  Pallas kernels  23.3 us (10%)
  starting transfers between devices  21.8 us (9%)
  between operations  14.7 us (6%)
  other arithmetic  13 us (6%)
  local copies, waits for them, and re-layouts  10.7 us (5%)
  matrix products  8.72 us (4%)
    all_to_all x5, blocking collectives, swap(): return lax.all_to_all(array, axes, split_axis=0, concat_axis=0, tiled=True)  76.8 us
    all_gather x1, blocking collectives, body(): share = lax.all_gather(share, YX, axis=0, tiled=False)  25.5 us
    pallas_call x1, Pallas kernels, attend(): pl.pallas_call(attend_kernel, grid=(sources // chunk,), in_specs=[pl.Bloc...  21.3 us
    all_gather x1, waiting for transfers between devices, body(): share = lax.all_gather(share, 'z', axis=0, tiled=False)  21 us
    all_to_all x3, starting transfers between devices, swap(): return lax.all_to_all(array, axes, split_axis=0, concat_axis=0, tiled=True)  13.6 us
    all_to_all x3, waiting for transfers between devices, swap(): return lax.all_to_all(array, axes, split_axis=0, concat_axis=0, tiled=True)  13.1 us
    ppermute x2, starting transfers between devices, neighbours(): before = lax.ppermute(tail, SEQ, [(i, i + 1) for i in range(count - 1)])  5.35 us
  transfers between devices with their start and end apart: 9, of which 5 were waited for; matrix products, arithmetic and copies ran while one was open for 7% of the time, Pallas kernels for 10%

profile of v1, /device:TPU:1, one launch (start us, length us, event | category | flops | bytes accessed | tf_op | source)
XLA Modules:
  0.0 232.2 jit_solution(4701389153943166881)
XLA Ops:
  7.2 0.9 dynamic-slice_bitcast_fusion
  8.1 25.5 %all-gather = bf16[256,512]{1,0:T(8,128)(2,1)} all-gather(bf16[32,512]{1,0:T(8,128)(2,1)S(1)} %dynamic-slice_bitcast_fusion), channel_id=2, replica_groups=mesh['yh'=4,'core'=2,'yl'=2,'x'=4,'z'=8] {'yl','x'}, dimensions={0}, use_global_device_ids=true | all-gather | bytes 294912 | tf_op jit(solution)/shard_map/all_gather | solution.py:181
  33.7 2.0 shard_map.129
  35.7 20.8 %all_to_all.40 = bf16[8,3,64,128]{3,2,1,0:T(8,128)(2,1)S(1)} all-to-all(bf16[8,3,64,128]{3,2,1,0:T(8,128)(2,1)} %shard_map.129), channel_id=1, replica_groups=mesh['yh'=4,'core'=2,'yl'=2,'x'=4,'z'=8] {'z'}, dimensions={0} | all-to-all | bytes 786432 | tf_op jit(solution)/shard_map/all_to_all | solution.py:125
  56.5 1.9 broadcast_in_dim.14
  58.4 4.4 %all-to-all-start.1 = ((bf16[8,8,2,64,128]{4,3,2,1,0:T(8,128)(2,1)}), bf16[8,8,2,64,128]{4,3,2,1,0:T(8,128)(2,1)}, u32[]{:S(2)}, u32[]{:S(2)}) async-start(bf16[8,8,2,64,128]{4,3,2,1,0:T(8,128)(2,1)} %broadcast_in_dim.14), calls=%async_computation.1 | async-start | bytes 4194304 | tf_op jit(solution)/shard_map/all_to_all | solution.py:125
  62.9 21.0 %all-gather.6.cloned.1.call-done = bf16[64,32,512]{2,1,0:T(8,128)(2,1)} async-done(((bf16[8,32,512]{2,1,0:T(8,128)(2,1)}), bf16[64,32,512]{2,1,0:T(8,128)(2,1)}) %all-gather.6.cloned.1.call-update) | async-done | bytes 2097168 | tf_op jit(solution)/shard_map/all_gather | solution.py:182
  84.5 3.5 %all-to-all-done.1 = bf16[8,8,2,64,128]{4,3,2,1,0:T(8,128)(2,1)} async-done(((bf16[8,8,2,64,128]{4,3,2,1,0:T(8,128)(2,1)}), bf16[8,8,2,64,128]{4,3,2,1,0:T(8,128)(2,1)}, u32[]{:S(2)}, u32[]{:S(2)}) %all-to-all-start.1) | async-done | bytes 2097184 | tf_op jit(solution)/shard_map/all_to_all | solution.py:125
  88.0 21.3 %shard_map.130 = bf16[8,64,128]{2,1,0:T(8,128)(2,1)} custom-call(bf16[8,64,128]{2,1,0:T(8,128)(2,1)} %slice_bitcast_fusion.q_ref, bf16[64,2,64,128]{3,2,1,0:T(8,128)(2,1)} %bitcast.5.kv_ref), custom_call_target="tpu_custom_call" | custom-call | tf_op jit(solution)/shard_map/pallas_call | solution.py:105
  109.3 3.5 %all-to-all-start.2 = ((bf16[8,64,128]{2,1,0:T(8,128)(2,1)}), bf16[8,64,128]{2,1,0:T(8,128)(2,1)S(1)}, u32[]{:S(2)}, u32[]{:S(2)}) async-start(bf16[8,64,128]{2,1,0:T(8,128)(2,1)} %shard_map.130), calls=%async_computation.2 | async-start | bytes 262144 | tf_op jit(solution)/shard_map/all_to_all | solution.py:125
  112.9 3.3 %collective-permute-start.2 = (bf16[15,1024]{1,0:T(8,128)(2,1)S(1)}, bf16[15,1024]{1,0:T(8,128)(2,1)S(1)}, u32[]{:S(2)}, u32[]{:S(2)}) collective-permute-start(bf16[15,1024]{1,0:T(8,128)(2,1)S(1)} %get-tuple-element.46), channel_id=1, source_target_pairs={{0,1},{1,2},{2,3},{3,4},{4,5},{5,6},{6,7},{7,8},{8,9},{9,10},{10,1... | collective-permute-start | bytes 92168 | tf_op jit(solution)/shard_map/ppermute | solution.py:136
  116.1 1.3 collective-permute-start.3
  117.5 3.3 %all-to-all-done.2 = bf16[8,64,128]{2,1,0:T(8,128)(2,1)S(1)} async-done(((bf16[8,64,128]{2,1,0:T(8,128)(2,1)}), bf16[8,64,128]{2,1,0:T(8,128)(2,1)S(1)}, u32[]{:S(2)}, u32[]{:S(2)}) %all-to-all-start.2) | async-done | bytes 131104 | tf_op jit(solution)/shard_map/all_to_all | solution.py:125
  120.8 1.6 fusion.108
  122.9 2.5 %fusion.106 = (bf16[8,8,32,512]{3,2,1,0:T(8,128)(2,1)S(1)}, bf16[8,8,32,512]{3,2,1,0:T(8,128)(2,1)S(1)}) fusion(bf16[16,8,32,512]{3,2,1,0:T(8,128)(2,1)} %all-gather.8.cloned.1.call-done), kind=kLoop, calls=%fused_computation.237 | loop fusion | bytes 8388608 | tf_op jit(solution)/shard_map/slice | solution.py:185
  126.7 0.8 convolution_add_fusion
  127.7 2.1 collective-permute-start
  129.8 1.5 collective-permute-start.1
  131.3 3.5 %collective-permute-done.1 = bf16[30,1024]{1,0:T(8,128)(2,1)S(1)} collective-permute-done((bf16[30,1024]{1,0:T(8,128)(2,1)S(1)}, bf16[30,1024]{1,0:T(8,128)(2,1)S(1)}, u32[]{:S(2)}, u32[]{:S(2)}) %collective-permute-start.1) | collective-permute-done | bytes 61472 | tf_op jit(solution)/shard_map/ppermute | solution.py:137
  134.9 3.6 %add_divide_fusion = (f32[158,1024]{1,0:T(8,128)}, f32[158,1024]{1,0:T(8,128)S(1)}) fusion(bf16[30,1024]{1,0:T(8,128)(2,1)S(1)} %collective-permute-done.1, bf16[128,1024]{1,0:T(8,128)(2,1)S(1)} %multiply_convert_fusion.2, f32[1024]{0:T(1024)S(1)} %bitcast.158, bf16[188,1024]{1,0:T(8,128)(2,1)S(1)} %pad_maximum_fusion.5, f32[1024]{0:T(1024)S(1)} %bitcast.160, ...), kind=kLoop, calls=%fused_computation.82 | loop fusion | flops 16340992 | bytes 11190272 | tf_op jit(solution)/shard_map/div | solution.py:214
  138.5 1.7 fusion.2
  140.2 2.3 multiply_convert_fusion.1
  147.2 1.2 add_convert_fusion
  148.9 1.1 copy.56
  150.0 1.4 pad_maximum_fusion.2
  151.7 9.2 %all_to_all.41 = bf16[2,272,1024]{2,1,0:T(8,128)(2,1)S(1)} all-to-all(bf16[2,272,1024]{2,1,0:T(8,128)(2,1)S(1)} %copy.58), channel_id=1, replica_groups=mesh['yh'=4,'core'=2,'yl'=2,'x'=4,'z'=8] {'core'}, dimensions={0} | all-to-all | bytes 2228224 | tf_op jit(solution)/shard_map/all_to_all | solution.py:125
  161.3 18.2 %all_to_all.42 = bf16[8,48,1024]{2,1,0:T(8,128)(2,1)S(1)} all-to-all(bf16[8,48,1024]{2,1,0:T(8,128)(2,1)S(1)} %pad_maximum_fusion.3), channel_id=1, replica_groups=mesh['yh'=4,'core'=2,'yl'=2,'x'=4,'z'=8] {'yl','x'}, dimensions={0} | all-to-all | bytes 1572864 | tf_op jit(solution)/shard_map/all_to_all | solution.py:125
  179.9 18.0 %all_to_all.43 = bf16[8,20,1024]{2,1,0:T(8,128)(2,1)S(1)} all-to-all(bf16[8,20,1024]{2,1,0:T(8,128)(2,1)S(1)} %pad_maximum_fusion.6), channel_id=1, replica_groups=mesh['yh'=4,'core'=2,'yl'=2,'x'=4,'z'=8] {'z'}, dimensions={0} | all-to-all | bytes 655360 | tf_op jit(solution)/shard_map/all_to_all | solution.py:125
  199.1 5.7 %all-to-all-start.6 = ((f32[4,20,1024]{2,1,0:T(8,128)}), f32[4,20,1024]{2,1,0:T(8,128)S(1)}, u32[]{:S(2)}, u32[]{:S(2)}) async-start(f32[4,20,1024]{2,1,0:T(8,128)} %broadcast_in_dim.19), calls=%async_computation.6 | async-start | bytes 786432 | tf_op jit(solution)/shard_map/all_to_all | solution.py:125
  204.8 2.4 %fusion.6 = bf16[1,128,1024]{2,1,0:T(8,128)(2,1)} fusion(f32[128,1024]{1,0:T(8,128)S(1)} %get-tuple-element.82, bf16[1024,1024]{1,0:T(8,128)(2,1)S(1)} %copy-done, f32[158,1024]{1,0:T(8,128)} %get-tuple-element.41, f32[158,1024]{1,0:T(8,128)} %copy-done.2), kind=kOutput, calls=%fused_computation.77 | convolution fusion | flops 268959744 | bytes 3932160 | tf_op jit(solution)/shard_map/dot_general | solution.py:216
  207.2 6.4 %all-to-all-done.6 = f32[4,20,1024]{2,1,0:T(8,128)S(1)} async-done(((f32[4,20,1024]{2,1,0:T(8,128)}), f32[4,20,1024]{2,1,0:T(8,128)S(1)}, u32[]{:S(2)}, u32[]{:S(2)}) %all-to-all-start.6) | async-done | bytes 327712 | tf_op jit(solution)/shard_map/all_to_all | solution.py:125
  213.6 10.5 %all_to_all.44 = f32[2,20,1024]{2,1,0:T(8,128)S(1)} all-to-all(f32[2,20,1024]{2,1,0:T(8,128)S(1)} %broadcast_in_dim.20), channel_id=1, replica_groups=mesh['yh'=4,'core'=2,'yl'=2,'x'=4,'z'=8] {'core'}, dimensions={0} | all-to-all | bytes 327680 | tf_op jit(solution)/shard_map/all_to_all | solution.py:125
  (101 shorter events, 11.2 us)
Async XLA Ops:
  7.2 131.3 %copy-start = (bf16[1024,1024]{1,0:T(8,128)(2,1)S(1)}, bf16[1024,1024]{1,0:T(8,128)(2,1)}, u32[]{:S(2)}) copy-start(bf16[1024,1024]{1,0:T(8,128)(2,1)} %param.16) | copy-start | bytes 6291460
  7.2 76.6 %all-gather.6.cloned.1.call-start = ((), (), s32[]{:S(2)}) async-start(), calls=%async_computation.8 | async-start | bytes 2359296 | tf_op jit(solution)/shard_map/all_gather | solution.py:182
  58.4 29.6 %all-to-all-start.1 = ((bf16[8,8,2,64,128]{4,3,2,1,0:T(8,128)(2,1)}), bf16[8,8,2,64,128]{4,3,2,1,0:T(8,128)(2,1)}, u32[]{:S(2)}, u32[]{:S(2)}) async-start(bf16[8,8,2,64,128]{4,3,2,1,0:T(8,128)(2,1)} %broadcast_in_dim.14), calls=%async_computation.1 | async-start | bytes 4194304 | tf_op jit(solution)/shard_map/all_to_all | solution.py:125
  62.8 60.0 %all-gather.8.cloned.1.call-start = ((), (), s32[]{:S(2)}) async-start(), calls=%async_computation.9 | async-start | bytes 6291456 | tf_op jit(solution)/shard_map/all_gather | solution.py:183
  83.8 29.0 %copy-start.3 = (bf16[1,128,1024]{2,1,0:T(8,128)(2,1)S(1)}, bf16[1,128,1024]{2,1,0:T(8,128)(2,1)}, u32[]{:S(2)}) copy-start(bf16[1,128,1024]{2,1,0:T(8,128)(2,1)} %param.19) | copy-start | bytes 786436
  83.8 33.6 %copy-start.5 = (bf16[31,1024]{1,0:T(8,128)(2,1)S(1)}, bf16[31,1024]{1,0:T(8,128)(2,1)}, u32[]{:S(2)}) copy-start(bf16[31,1024]{1,0:T(8,128)(2,1)} %param.17) | copy-start | bytes 190468
  83.8 37.0 %copy-start.4 = (bf16[1,128,1024]{2,1,0:T(8,128)(2,1)S(1)}, bf16[1,128,1024]{2,1,0:T(8,128)(2,1)}, u32[]{:S(2)}) copy-start(bf16[1,128,1024]{2,1,0:T(8,128)(2,1)} %param.13) | copy-start | bytes 786436
  109.3 13.3 %copy-start.6 = (f32[1024]{0:T(1024)S(1)}, f32[1024]{0:T(1024)}, u32[]{:S(2)}) copy-start(f32[1024]{0:T(1024)} %param.18) | copy-start | bytes 12292
  109.3 11.5 %all-to-all-start.2 = ((bf16[8,64,128]{2,1,0:T(8,128)(2,1)}), bf16[8,64,128]{2,1,0:T(8,128)(2,1)S(1)}, u32[]{:S(2)}, u32[]{:S(2)}) async-start(bf16[8,64,128]{2,1,0:T(8,128)(2,1)} %shard_map.130), calls=%async_computation.2 | async-start | bytes 262144 | tf_op jit(solution)/shard_map/all_to_all | solution.py:125
  112.9 25.6 %collective-permute-start.2 = (bf16[15,1024]{1,0:T(8,128)(2,1)S(1)}, bf16[15,1024]{1,0:T(8,128)(2,1)S(1)}, u32[]{:S(2)}, u32[]{:S(2)}) collective-permute-start(bf16[15,1024]{1,0:T(8,128)(2,1)S(1)} %get-tuple-element.46), channel_id=1, source_target_pairs={{0,1},{1,2},{2,3},{3,4},{4,5},{5,6},{6,7},{7,8},{8,9},{9,10},{10,1... | collective-permute-start | bytes 92168 | tf_op jit(solution)/shard_map/ppermute | solution.py:136
  116.1 22.3 %collective-permute-start.3 = (bf16[15,1024]{1,0:T(8,128)(2,1)S(1)}, bf16[15,1024]{1,0:T(8,128)(2,1)}, u32[]{:S(2)}, u32[]{:S(2)}) collective-permute-start(bf16[15,1024]{1,0:T(8,128)(2,1)S(1)} %get-tuple-element.47), channel_id=1, source_target_pairs={{1,0},{2,1},{3,2},{4,3},{5,4},{6,5},{7,6},{8,7},{9,8},{10,9},{11,1... | collective-permute-start | bytes 92168 | tf_op jit(solution)/shard_map/ppermute | solution.py:137
  127.7 3.6 %collective-permute-start = (bf16[30,1024]{1,0:T(8,128)(2,1)S(1)}, bf16[30,1024]{1,0:T(8,128)(2,1)S(1)}, u32[]{:S(2)}, u32[]{:S(2)}) collective-permute-start(bf16[30,1024]{1,0:T(8,128)(2,1)S(1)} %get-tuple-element.48), channel_id=1, source_target_pairs={{0,1},{1,2},{2,3},{3,4},{4,5},{5,6},{6,7},{7,8},{8,9},{9,10},{10,1... | collective-permute-start | bytes 184328 | tf_op jit(solution)/shard_map/ppermute | solution.py:136
  129.8 5.0 %collective-permute-start.1 = (bf16[30,1024]{1,0:T(8,128)(2,1)S(1)}, bf16[30,1024]{1,0:T(8,128)(2,1)S(1)}, u32[]{:S(2)}, u32[]{:S(2)}) collective-permute-start(bf16[30,1024]{1,0:T(8,128)(2,1)S(1)} %get-tuple-element.49), channel_id=1, source_target_pairs={{1,0},{2,1},{3,2},{4,3},{5,4},{6,5},{7,6},{8,7},{9,8},{10,9},{11,1... | collective-permute-start | bytes 184328 | tf_op jit(solution)/shard_map/ppermute | solution.py:137
  138.5 1.7 copy-start.2
  148.4 3.0 %copy-start.1 = (bf16[128,1024]{1,0:T(8,128)(2,1)}, bf16[128,1024]{1,0:T(8,128)(2,1)S(1)}, u32[]{:S(2)}) copy-start(bf16[128,1024]{1,0:T(8,128)(2,1)S(1)} %add_convert_fusion) | copy-start | bytes 786436
  199.1 14.5 %all-to-all-start.6 = ((f32[4,20,1024]{2,1,0:T(8,128)}), f32[4,20,1024]{2,1,0:T(8,128)S(1)}, u32[]{:S(2)}, u32[]{:S(2)}) async-start(f32[4,20,1024]{2,1,0:T(8,128)} %broadcast_in_dim.19), calls=%async_computation.6 | async-start | bytes 786432 | tf_op jit(solution)/shard_map/all_to_all | solution.py:125
Sparse Core Ops, SparseCore 0:
  33.8 49.9 all-gather.5
  85.9 25.5 all-gather.7

commit v2 on v1

v2 whole, which is shorter than its diff:
```python
import math

import jax
import jax.numpy as jnp
from jax import lax
from jax.experimental import pallas as pl
from jax.experimental.pallas import tpu as pltpu
from jax.sharding import Mesh, PartitionSpec as P


HEADS = 8
DH = 64
KW = 31
norm_epsilon = 1e-05

F32 = jnp.float32
BF16 = jnp.bfloat16

YX = ("yl", "x")
SEQ = ("yl", "x", "z")
NT = (((1,), (1,)), ((), ()))


def pack_kernel(q_ref, k_ref, v_ref, w_ref, o_ref):
    for pair in range(HEADS // 2):
        cols = pl.ds(pair * 128, 128)
        q_t = q_ref[:, cols].astype(F32).T.astype(BF16)
        v_t = v_ref[:, cols].astype(F32).T.astype(BF16)
        upper = k_ref[0:64, cols].astype(F32)
        lower = k_ref[64:128, cols].astype(F32)
        lane = lax.broadcasted_iota(jnp.int32, upper.shape, 1)
        first = jnp.where(lane < 64, upper, pltpu.roll(lower, 64, 1)).astype(BF16)
        second = jnp.where(lane < 64, pltpu.roll(upper, 64, 1), lower).astype(BF16)
        for half, packed in ((0, first), (1, second)):
            head = 2 * pair + half
            o_ref[head, 0] = q_t[half * 64 : half * 64 + 64]
            o_ref[head, 1] = packed
            o_ref[head, 2] = v_t[half * 64 : half * 64 + 64]
    for half in range(2):
        turned = jnp.concatenate(
            [
                w_ref[half * 256 + b * 128 : half * 256 + b * 128 + 128, :].astype(F32).T
                for b in range(2)
            ],
            axis=0,
        ).astype(BF16)
        for head in range(HEADS):
            o_ref[head, 3 + half] = turned


def pack(q, k, v, w):
    return pl.pallas_call(
        pack_kernel,
        out_shape=jax.ShapeDtypeStruct((HEADS, 5, 64, 128), BF16),
    )(q, k, v, w)


SCALE = DH ** (-0.5) * math.log2(math.e)
QB = 256
SMALLEST = 2.0**-90
COST = pl.CostEstimate(flops=2**34, transcendentals=2**23, bytes_accessed=2**21)


def block_of(kv_ref, start, sources):
    packed = kv_ref[pl.ds(start, sources), 0].reshape(sources * 64, 128)
    keys = jnp.concatenate([packed, packed], axis=1)
    values = jnp.concatenate([kv_ref[start + s, 1] for s in range(sources)], axis=1)
    return keys, jnp.concatenate([values, jnp.ones((16, sources * 128), BF16)], axis=0)


def interleave(p_lo, p_hi, sources):
    pieces = []
    for s in range(sources):
        pieces.append(p_lo[s * 64 : s * 64 + 64])
        pieces.append(p_hi[s * 64 : s * 64 + 64])
    return jnp.concatenate(pieces, axis=0)


def attend_kernel(q_ref, kv_ref, o_ref, r_lo, r_hi, top, acc):
    count = q_ref.shape[0]
    sources = kv_ref.shape[0]
    blocks = count * 128 // QB
    group = 16
    whole = sources

    lane = lax.broadcasted_iota(jnp.int32, (128, 128), 1) < 64
    row = lax.broadcasted_iota(jnp.int32, (128, 128), 0) < 64
    same = (lane == row).astype(BF16)

    def longest(i, so_far):
        wide = kv_ref[pl.ds(i * group, group), 0].reshape(group * 64, 128).astype(F32)
        squares = (wide * wide).astype(BF16)
        return jnp.maximum(
            so_far,
            jnp.max(jnp.dot(squares, same, preferred_element_type=F32), axis=0, keepdims=True),
        )

    key_square = jnp.max(
        lax.fori_loop(0, sources // group, longest, jnp.zeros((1, 128), F32)),
        axis=1,
        keepdims=True,
    ) * 1.02

    for i in range(count):
        scaled = q_ref[i].astype(F32) * SCALE
        high = scaled.astype(BF16)
        low = (scaled - high.astype(F32)).astype(BF16)
        none = jnp.zeros_like(high)
        cols = pl.ds(i * 128, 128)
        r_lo[:, cols] = jnp.concatenate([high, none, low, none], axis=0)
        r_hi[:, cols] = jnp.concatenate([none, high, none, low], axis=0)
        top[:, cols] = jnp.sqrt(jnp.sum(scaled * scaled, axis=0, keepdims=True) * key_square)
    acc[...] = jnp.zeros(acc.shape, F32)

    def direct(i, carry):
        keys, values = block_of(kv_ref, i * whole, whole)
        for block in range(blocks):
            cols = pl.ds(block * QB, QB)
            bound = top[:, cols]
            s_lo = jnp.dot(keys, r_lo[:, cols], preferred_element_type=F32)
            p_lo = jnp.exp2(s_lo - bound).astype(BF16)
            s_hi = jnp.dot(keys, r_hi[:, cols], preferred_element_type=F32)
            p_hi = jnp.exp2(s_hi - bound).astype(BF16)
            acc[:, cols] += jnp.dot(
                values, interleave(p_lo, p_hi, whole), preferred_element_type=F32
            )
        return carry

    lax.fori_loop(0, sources // whole, direct, 0)

    @pl.when(jnp.min(acc[64:65]) < SMALLEST)
    def _():
        top[...] = jnp.full(top.shape, -jnp.inf, F32)
        acc[...] = jnp.zeros(acc.shape, F32)

        def online(i, carry):
            keys, values = block_of(kv_ref, i, 1)
            for block in range(blocks):
                cols = pl.ds(block * QB, QB)
                s_lo = jnp.dot(keys, r_lo[:, cols], preferred_element_type=F32)
                s_hi = jnp.dot(keys, r_hi[:, cols], preferred_element_type=F32)
                before = top[:, cols]
                highest = jnp.maximum(
                    before, jnp.max(jnp.maximum(s_lo, s_hi), axis=0, keepdims=True)
                )
                top[:, cols] = highest
                p_lo = jnp.exp2(s_lo - highest).astype(BF16)
                p_hi = jnp.exp2(s_hi - highest).astype(BF16)
                mixed = jnp.dot(values, interleave(p_lo, p_hi, 1), preferred_element_type=F32)
                acc[:, cols] = acc[:, cols] * jnp.exp2(before - highest) + mixed
            return carry

        lax.fori_loop(0, sources, online, 0)

    done = (acc[0:64] / acc[64:65]).astype(BF16)
    for i in range(count):
        o_ref[i] = done[:, i * 128 : i * 128 + 128]


def attend(q_t, kv):
    count = q_t.shape[0]
    return pl.pallas_call(
        attend_kernel,
        out_shape=jax.ShapeDtypeStruct((count, 64, 128), BF16),
        scratch_shapes=[
            pltpu.VMEM((256, count * 128), BF16),
            pltpu.VMEM((256, count * 128), BF16),
            pltpu.VMEM((1, count * 128), F32),
            pltpu.VMEM((80, count * 128), F32),
        ],
        cost_estimate=COST,
        compiler_params=pltpu.CompilerParams(vmem_limit_bytes=56 * 1024 * 1024),
    )(q_t, kv)


STEPS = 4


def columns_of(w_ref, half):
    count = w_ref.shape[1] * 32
    return jnp.concatenate(
        [w_ref[half, :, b].reshape(count, 128) for b in range(4)], axis=1
    )


def gate_kernel(
    core_ref, att_ref, out_proj_ref, residual_ref, gain_ref, cot_ref, own_ref, other_ref,
    mid_ref, hat_ref, rscale_ref, value_ref, gate_ref, gated_ref, first_ref, last_ref, normed,
):
    step = pl.program_id(0)
    core = core_ref[0]
    half = normed.shape[2]

    @pl.when(step == 0)
    def _():
        att = att_ref[...].astype(F32).T.astype(BF16)
        mid = (
            residual_ref[...].astype(F32)
            + jnp.dot(att, out_proj_ref[...], preferred_element_type=F32)
        ).astype(BF16)
        mid_ref[...] = mid
        wide = mid.astype(F32)
        centered = wide - jnp.mean(wide, axis=1, keepdims=True)
        rscale = lax.rsqrt(jnp.mean(centered * centered, axis=1, keepdims=True) + norm_epsilon)
        hat = centered * rscale
        hat_ref[...] = hat
        rscale_ref[...] = jnp.broadcast_to(rscale, rscale_ref.shape)
        scaled = (hat * gain_ref[...]).astype(BF16)
        normed[0] = scaled[:, :half]
        normed[1] = scaled[:, half:]

    def project(part):
        return lax.dot_general(
            normed[core], columns_of(own_ref, part), NT, preferred_element_type=F32
        ) + lax.dot_general(
            normed[1 - core], columns_of(other_ref, part), NT, preferred_element_type=F32
        )

    value = project(0)
    gate = jax.nn.sigmoid(project(1))
    value_ref[...] = value
    gate_ref[...] = gate
    gated = (value * gate).astype(BF16)
    gated_ref[...] = gated
    rows = gated.shape[0]
    first_ref[0:32] = gated[0:32]
    first_ref[32:48] = cot_ref[0:16]
    last_ref[0:32] = gated[rows - 32 :]
    last_ref[32:48] = cot_ref[rows - 16 :]


def gate(core, att, out_proj, residual, gain, cot, own, other):
    rows, model = residual.shape
    part = model // STEPS
    whole = lambda *shape: pl.BlockSpec(shape, lambda i: (0,) * len(shape))
    block = lambda count: pl.BlockSpec((count, part), lambda i: (0, i))
    weights = pl.BlockSpec((2, part // 32, 4, 32, 128), lambda i: (0, i, 0, 0, 0))
    array = jax.ShapeDtypeStruct
    return pl.pallas_call(
        gate_kernel,
        grid=(STEPS,),
        in_specs=[
            pl.BlockSpec(memory_space=pltpu.SMEM),
            whole(*att.shape),
            whole(*out_proj.shape),
            whole(rows, model),
            whole(1, model),
            block(rows),
            weights,
            weights,
        ],
        out_specs=[
            whole(rows, model),
            whole(rows, model),
            whole(rows, 128),
            block(rows),
            block(rows),
            block(rows),
            block(48),
            block(48),
        ],
        out_shape=[
            array((rows, model), BF16),
            array((rows, model), F32),
            array((rows, 128), F32),
            array((rows, model), F32),
            array((rows, model), F32),
            array((rows, model), BF16),
            array((48, model), BF16),
            array((48, model), BF16),
        ],
        scratch_shapes=[pltpu.VMEM((2, rows, model // 2), BF16)],
        compiler_params=pltpu.CompilerParams(vmem_limit_bytes=56 * 1024 * 1024),
    )(core, att, out_proj, residual, gain, cot, own, other)


def back_kernel(
    core_ref, before_ref, after_ref, gated_ref, cot_before_ref, cot_after_ref, cot_ref,
    conv_out_ref, taps_ref, value_ref, gate_ref, own_ref, other_ref, mid_ref, hat_ref, rscale_ref,
    gain_ref, att_ref,
    layer_ref, grad_mid_ref, sums_ref,
    cot_wide, padded, gradient, layer_sum, normed_grad,
):
    step = pl.program_id(0)
    core = core_ref[0]
    rows = gated_ref.shape[0]
    tiles = padded.shape[0]

    @pl.when(step == 0)
    def _():
        cot_wide[0:16] = cot_before_ref[32:48]
        cot_wide[16 : 16 + rows] = cot_ref[...]
        cot_wide[16 + rows : 32 + rows] = cot_after_ref[32:48]
        layer_sum[...] = jnp.zeros(layer_sum.shape, F32)
        normed_grad[...] = jnp.zeros(normed_grad.shape, F32)

    for t in range(tiles):
        lanes = slice(t * 128, t * 128 + 128)
        padded[t, 0:32] = before_ref[0:32, lanes].astype(F32)
        padded[t, 32 : 32 + rows] = gated_ref[:, lanes].astype(F32)
        padded[t, 32 + rows : 64 + rows] = after_ref[0:32, lanes].astype(F32)

    weights = conv_out_ref[...]
    grad_act = lax.dot_general(cot_wide[...], weights, NT, preferred_element_type=F32)
    acts = []
    chunk = (rows + 32) // 2
    for t in range(tiles):
        lanes = slice(t * 128, t * 128 + 128)
        pieces = []
        for part in range(2):
            begin = part * chunk
            conv = jnp.zeros((chunk, 128), F32)
            for k in range(KW):
                conv = conv + taps_ref[k : k + 1, lanes] * padded[t, pl.ds(begin + k + 1, chunk)]
            sig = jax.nn.sigmoid(conv)
            pieces.append(conv * sig)
            gradient[t, begin : begin + chunk] = (
                (grad_act[begin : begin + chunk, lanes] * sig * (1.0 + conv * (1.0 - sig)))
                .astype(BF16)
                .astype(F32)
            )
        acts.append(jnp.concatenate(pieces, axis=0)[16 : 16 + rows])
    act = jnp.concatenate(acts, axis=1).astype(BF16)
    layer_sum[...] += jnp.dot(act, weights, preferred_element_type=F32)

    gated_grads = []
    for t in range(tiles):
        lanes = slice(t * 128, t * 128 + 128)
        pieces = []
        for part in range(2):
            begin = part * (rows // 2)
            total = jnp.zeros((rows // 2, 128), F32)
            for k in range(KW):
                total = total + taps_ref[k : k + 1, lanes] * gradient[
                    t, pl.ds(begin + 31 - k, rows // 2)
                ]
            pieces.append(total)
        gated_grads.append(jnp.concatenate(pieces, axis=0))

        inner = gradient[t, 16 : 16 + rows]
        terms = []
        for k in range(KW):
            terms.append(
                jnp.sum(padded[t, pl.ds(k + 17, rows)] * inner, axis=0, keepdims=True)
            )
        terms.append(jnp.zeros((1, 128), F32))
        tile = step * tiles + t
        sums_ref[tile // 4, 64:68, tile % 4] = (
            jnp.concatenate(terms, axis=0).astype(BF16).reshape(4, 8, 128)
        )

    grad_gated = jnp.concatenate(gated_grads, axis=1)
    value = value_ref[...]
    gate = gate_ref[...]
    to_value = (grad_gated * gate).astype(BF16)
    to_gate = (grad_gated * value * gate * (1.0 - gate)).astype(BF16)
    for place, ref in ((core, own_ref), (1 - core, other_ref)):
        normed_grad[place] += jnp.dot(
            to_value, columns_of(ref, 0), preferred_element_type=F32
        ) + jnp.dot(to_gate, columns_of(ref, 1), preferred_element_type=F32)

    @pl.when(step == pl.num_programs(0) - 1)
    def _():
        layer_ref[...] = (mid_ref[...].astype(F32) + layer_sum[...]).astype(BF16)
        hat = hat_ref[...]
        scaled = jnp.concatenate([normed_grad[0], normed_grad[1]], axis=1) * gain_ref[...]
        inner = (
            scaled
            - jnp.mean(scaled, axis=1, keepdims=True)
            - hat * jnp.mean(scaled * hat, axis=1, keepdims=True)
        )
        grad_mid = (cot_ref_f32(cot_ref) + rscale_ref[:, 0:1] * inner).astype(BF16)
        grad_mid_ref[...] = grad_mid
        for c in range(2):
            for b in range(4):
                cols = slice(c * 512 + b * 128, c * 512 + b * 128 + 128)
                product = jnp.dot(att_ref[...], grad_mid[:, cols], preferred_element_type=F32)
                sums_ref[c, 0:64, b] = product.astype(BF16).reshape(64, 8, 128)


def cot_ref_f32(ref):
    return ref[...].astype(F32)


def back(core, before, after, gated, cot, conv_out, taps, value, gate_half, own, other, mid, hat,
         rscale, gain, att):
    rows, model = gated.shape
    part = model // STEPS
    whole = lambda *shape: pl.BlockSpec(shape, lambda i: (0,) * len(shape))
    block = lambda count: pl.BlockSpec((count, part), lambda i: (0, i))
    weights = pl.BlockSpec((2, part // 32, 4, 32, 128), lambda i: (0, i, 0, 0, 0))
    array = jax.ShapeDtypeStruct
    return pl.pallas_call(
        back_kernel,
        grid=(STEPS,),
        in_specs=[
            pl.BlockSpec(memory_space=pltpu.SMEM),
            block(48),
            block(48),
            block(rows),
            whole(48, model),
            whole(48, model),
            whole(rows, model),
            pl.BlockSpec((part, model), lambda i: (i, 0)),
            block(KW + 1),
            block(rows),
            block(rows),
            weights,
            weights,
            whole(rows, model),
            whole(rows, model),
            whole(rows, 128),
            whole(1, model),
            whole(*att.shape),
        ],
        out_specs=[
            whole(rows, model),
            whole(rows, model),
            whole(2, 68, 4, 8, 128),
        ],
        out_shape=[
            array((rows, model), BF16),
            array((rows, model), BF16),
            array((2, 68, 4, 8, 128), BF16),
        ],
        scratch_shapes=[
            pltpu.VMEM((rows + 32, model), BF16),
            pltpu.VMEM((part // 128, rows + 64, 128), F32),
            pltpu.VMEM((part // 128, rows + 32, 128), F32),
            pltpu.VMEM((rows, model), F32),
            pltpu.VMEM((2, rows, model // 2), F32),
        ],
        compiler_params=pltpu.CompilerParams(vmem_limit_bytes=56 * 1024 * 1024),
    )(core, before, after, gated, before, after, cot, conv_out, taps, value, gate_half, own, other,
      mid, hat, rscale, gain, att)


def swap(array, axes):
    return lax.all_to_all(array, axes, split_axis=0, concat_axis=0, tiled=True)


def spread(array, axes, count):
    return swap(jnp.broadcast_to(array[None], (count,) + array.shape), axes)


def body(
    queries, keys, values, residual, out_proj, conv_in, conv_out, depth_kernel, norm_gain, cotangent
):
    rows = queries.shape[1]
    model = residual.shape[2]
    core = lax.axis_index("core")
    place = core.astype(jnp.int32).reshape(1)
    gain = norm_gain.reshape(1, model)
    cot = cotangent[0]
    taps = jnp.pad(depth_kernel.astype(F32), ((0, 1), (0, 0)))

    share = lax.dynamic_slice_in_dim(conv_in, core * (model // 2), model // 2, axis=0)
    sent = pack(queries[0], keys[0], values[0], share)
    got = swap(sent, "z")
    kv = spread(got[:, 1:3], YX, 8).reshape(64, 2, 64, 128)
    own = spread(got[:, 3:5], YX, 8).reshape(2, 32, 4, 32, 128)
    attended = attend(got[:, 0], kv)
    other = lax.ppermute(own, "core", [(0, 1), (1, 0)])
    att = swap(attended, "z").reshape(HEADS * DH, rows)

    mid, hat, rscale, value_half, gate_half, gated, first, last = gate(
        place, att, out_proj, residual[0], gain, cot, own, other
    )
    count = 64
    before = lax.ppermute(last, SEQ, [(i, i + 1) for i in range(count - 1)])
    after = lax.ppermute(first, SEQ, [(i + 1, i) for i in range(count - 1)])
    layer_out, grad_mid, sums = back(
        place, before, after, gated, cot, conv_out, taps, value_half, gate_half, own, other, mid,
        hat, rscale, gain, att,
    )

    sums = jnp.sum(swap(sums, "core").astype(F32), axis=0)

    def joined(array, width):
        first, second = array[: 8 * width], array[8 * width :]
        first = first.reshape((8, width) + array.shape[1:])
        second = jnp.broadcast_to(second[None], (8,) + second.shape)
        return jnp.concatenate([first, second], axis=1).astype(BF16)

    sums = jnp.sum(swap(joined(sums, 8), YX).astype(F32), axis=0)
    sums = jnp.sum(swap(joined(sums, 1), "z").astype(F32), axis=0)
    sums = jnp.sum(spread(sums.astype(BF16), "yh", 4).astype(F32), axis=0)
    sums = spread(sums, "core", 2)
    grad_out_proj = sums[:, 0].transpose(2, 0, 1, 3).reshape(8, model)
    grad_kernel = sums[:, 1:].transpose(1, 3, 0, 2, 4).reshape(32, model)[:KW]
    return layer_out[None], grad_mid[None], grad_out_proj, grad_kernel


def solution(mesh):
    split = Mesh(mesh.devices.reshape(4, 2, 2, 4, 8), ("yh", "core", "yl", "x", "z"))
    rows = P(("yh", "core"), SEQ, None)
    return jax.shard_map(
        body,
        mesh=split,
        in_specs=(rows, rows, rows, rows, P(), P(None, SEQ), P(), P(), P(), rows),
        out_specs=(rows, rows, P(SEQ, None), P()),
        check_vma=False,
    )
```

time: 233 us -> 276 us (1.18)
  Pallas kernels: 23.3 us -> 93.4 us
  blocking collectives: 102 us -> 137 us
  waiting for transfers between devices: 37.6 us -> 22.3 us
  between operations: 14.7 us -> 0.82 us
  other arithmetic: 13 us -> 1.13 us
  matrix products: 8.72 us -> 0 us
  starting transfers between devices: 21.8 us -> 13.6 us
  local copies, waits for them, and re-layouts: 10.7 us -> 6.9 us
    pallas_call x2 -> x4, Pallas kernels: 23.3 us -> 93.4 us  [the longest x1 74.2 us: attend(): pl.pallas_call(attend_kernel, out_shape=jax.ShapeDtypeStruct((count, 64,...]
    all_to_all x5 -> x8, blocking collectives: 76.8 us -> 137 us  [swap(): return lax.all_to_all(array, axes, split_axis=0, concat_axis=0, tiled=True)]
    all_gather x1 -> x0, blocking collectives: 25.5 us -> none  [body(): share = lax.all_gather(share, YX, axis=0, tiled=False)]
    all_gather x2 -> x0, waiting for transfers between devices: 21 us -> none  [the longest x1 21 us: body(): share = lax.all_gather(share, 'z', axis=0, tiled=False)]
    all_to_all x3 -> x1, starting transfers between devices: 13.6 us -> 4.34 us  [swap(): return lax.all_to_all(array, axes, split_axis=0, concat_axis=0, tiled=True)]
    dot_general x8 -> x0, matrix products: 8.72 us -> none  [the longest x1 2.39 us: body(): jnp.dot(act, conv_out, preferred_element_type=F32)]
    all_to_all x3 -> x1, waiting for transfers between devices: 13.1 us -> 18.8 us  [swap(): return lax.all_to_all(array, axes, split_axis=0, concat_axis=0, tiled=True)]
    div x3 -> x0, other arithmetic: 3.58 us -> none  [the longest x1 3.57 us: body(): sig_conv = jax.nn.sigmoid(conv)]
  transfers between devices with their start and end apart: 9 -> 4, of which waited for: 5 -> 2; matrix products, arithmetic and copies ran while one was open for 7% -> 0% of each run, Pallas kernels for 10% -> 27%
where the time goes in v2:
time: 276 us
  blocking collectives  137 us (50%)
  Pallas kernels  93.4 us (34%)
  waiting for transfers between devices  22.3 us (8%)
  starting transfers between devices  13.6 us (5%)
  local copies, waits for them, and re-layouts  6.9 us (2%)
    all_to_all x8, blocking collectives, swap(): return lax.all_to_all(array, axes, split_axis=0, concat_axis=0, tiled=True)  137 us
    pallas_call x1, Pallas kernels, attend(): pl.pallas_call(attend_kernel, out_shape=jax.ShapeDtypeStruct((count, 64,...  74.2 us
    all_to_all x1, waiting for transfers between devices, swap(): return lax.all_to_all(array, axes, split_axis=0, concat_axis=0, tiled=True)  18.8 us
    pallas_call x1, Pallas kernels, back(): pl.pallas_call(back_kernel, grid=(STEPS,), in_specs=[pl.BlockSpec(memory_...  11.1 us
    pallas_call x1, Pallas kernels, gate(): pl.pallas_call(gate_kernel, grid=(STEPS,), in_specs=[pl.BlockSpec(memory_...  6.02 us
    ppermute x1, starting transfers between devices, body(): other = lax.ppermute(own, 'core', [(0, 1), (1, 0)])  5.7 us
  transfers between devices with their start and end apart: 4, of which 2 were waited for; matrix products, arithmetic and copies ran while one was open for 0% of the time, Pallas kernels for 27%

profile of v2, /device:TPU:1, one launch (start us, length us, event | category | flops | bytes accessed | tf_op | source)
XLA Modules:
  0.0 275.7 jit_solution(8571833060887946736)
XLA Ops:
  0.6 0.0 copy-start
  0.7 0.8 copy-done
  1.5 0.8 copy.30.w_ref
  2.2 2.1 shard_map.129
  4.4 30.1 %all_to_all.45 = bf16[8,5,64,128]{3,2,1,0:T(8,128)(2,1)S(1)} all-to-all(bf16[8,5,64,128]{3,2,1,0:T(8,128)(2,1)} %shard_map.129), channel_id=1, replica_groups=mesh['yh'=4,'core'=2,'yl'=2,'x'=4,'z'=8] {'z'}, dimensions={0} | all-to-all | bytes 1310720 | tf_op jit(solution)/shard_map/all_to_all | solution.py:439
  34.5 0.5 broadcast_in_dim.17
  35.0 29.1 %all_to_all.46 = bf16[8,8,2,64,128]{4,3,2,1,0:T(8,128)(2,1)S(1)} all-to-all(bf16[8,8,2,64,128]{4,3,2,1,0:T(8,128)(2,1)S(1)} %broadcast_in_dim.17), channel_id=1, replica_groups=mesh['yh'=4,'core'=2,'yl'=2,'x'=4,'z'=8] {'yl','x'}, dimensions={0} | all-to-all | bytes 4194304 | tf_op jit(solution)/shard_map/all_to_all | solution.py:439
  64.2 2.0 broadcast_in_dim.16
  66.1 4.3 %all-to-all-start.1 = ((bf16[8,8,2,64,128]{4,3,2,1,0:T(8,128)(2,1)}), bf16[8,8,2,64,128]{4,3,2,1,0:T(8,128)(2,1)}, u32[]{:S(2)}, u32[]{:S(2)}) async-start(bf16[8,8,2,64,128]{4,3,2,1,0:T(8,128)(2,1)} %broadcast_in_dim.16), calls=%async_computation.1 | async-start | bytes 4194304 | tf_op jit(solution)/shard_map/all_to_all | solution.py:439
  70.5 5.7 %collective-permute-start = (bf16[2,32,4,32,128]{4,3,2,1,0:T(8,128)(2,1)S(1)}, bf16[2,32,4,32,128]{4,3,2,1,0:T(8,128)(2,1)}, u32[]{:S(2)}, u32[]{:S(2)}) collective-permute-start(bf16[2,32,4,32,128]{4,3,2,1,0:T(8,128)(2,1)S(1)} %bitcast.30), channel_id=1, source_target_pairs={{0,64},{64,0},{1,65},{65,1},{2,66},{66,2},{3,67},{67,3},{4,68},{68... | collective-permute-start | bytes 6291464 | tf_op jit(solution)/shard_map/ppermute | solution.py:463
  76.2 0.7 slice_bitcast_fusion.q_ref
  76.9 18.8 %all-to-all-done.1 = bf16[8,8,2,64,128]{4,3,2,1,0:T(8,128)(2,1)} async-done(((bf16[8,8,2,64,128]{4,3,2,1,0:T(8,128)(2,1)}), bf16[8,8,2,64,128]{4,3,2,1,0:T(8,128)(2,1)}, u32[]{:S(2)}, u32[]{:S(2)}) %all-to-all-start.1) | async-done | bytes 2097184 | tf_op jit(solution)/shard_map/all_to_all | solution.py:439
  95.7 74.2 %shard_map.130 = bf16[8,64,128]{2,1,0:T(8,128)(2,1)} custom-call(bf16[8,64,128]{2,1,0:T(8,128)(2,1)} %slice_bitcast_fusion.q_ref, bf16[64,2,64,128]{3,2,1,0:T(8,128)(2,1)} %bitcast.5.kv_ref), custom_call_target="tpu_custom_call" | custom-call | flops 17179869184 | bytes 2097152 | tf_op jit(solution)/shard_map/pallas_call | solution.py:162
  169.9 12.4 %all_to_all.47 = bf16[8,64,128]{2,1,0:T(8,128)(2,1)} all-to-all(bf16[8,64,128]{2,1,0:T(8,128)(2,1)} %shard_map.130), channel_id=1, replica_groups=mesh['yh'=4,'core'=2,'yl'=2,'x'=4,'z'=8] {'z'}, dimensions={0} | all-to-all | bytes 262144 | tf_op jit(solution)/shard_map/all_to_all | solution.py:439
  182.3 0.0 collective-permute-done.other_ref
  182.3 6.0 %shard_map.131 = (bf16[128,1024]{1,0:T(8,128)(2,1)}, f32[128,1024]{1,0:T(8,128)}, f32[128,128]{1,0:T(8,128)}, f32[128,1024]{1,0:T(8,128)}, f32[128,1024]{1,0:T(8...) custom-call(s32[1]{0:T(128)} %bitcast.core_ref, bf16[512,128]{1,0:T(8,128)(2,1)} %bitcast.34, ...), custom_call_target="tpu_custom_call" | custom-call | tf_op jit(solution)/shard_map/pallas_call | solution.py:239
  188.3 2.1 collective-permute-start.1
  190.4 1.5 collective-permute-start.2
  191.9 0.7 pad_convert_fusion.taps_ref
  192.6 3.4 %collective-permute-done.2.after_ref.cot_after_ref = bf16[48,1024]{1,0:T(8,128)(2,1)S(1)} collective-permute-done((bf16[48,1024]{1,0:T(8,128)(2,1)}, bf16[48,1024]{1,0:T(8,128)(2,1)S(1)}, u32[]{:S(2)}, u32[]{:S(2)}) %collective-permute-start.2) | collective-permute-done | bytes 98336 | tf_op jit(solution)/shard_map/ppermute | solution.py:471
  196.0 0.6 copy-done.3
  196.6 11.1 %shard_map.132 = (bf16[128,1024]{1,0:T(8,128)(2,1)}, bf16[128,1024]{1,0:T(8,128)(2,1)}, bf16[2,68,4,8,128]{4,3,2,1,0:T(8,128)(2,1)}) custom-call(s32[1]{0:T(128)} %bitcast.core_ref, bf16[48,1024]{1,0:T(8,128)(2,1)} %copy-done.2, bf16[48,1024]{1,0:T(8,128)(2,1)} %copy-done.3, bf16[128,1024]{1,0:T(8,128)(2,1)} %get-tuple-element.17.gated_ref, ...), custom_call_target="tpu_custom_call" | custom-call | tf_op jit(solution)/shard_map/pallas_call | solution.py:393
  207.8 9.3 %all_to_all.48 = bf16[2,68,4,8,128]{4,3,2,1,0:T(8,128)(2,1)S(1)} all-to-all(bf16[2,68,4,8,128]{4,3,2,1,0:T(8,128)(2,1)} %get-tuple-element.25), channel_id=1, replica_groups=mesh['yh'=4,'core'=2,'yl'=2,'x'=4,'z'=8] {'core'}, dimensions={0} | all-to-all | bytes 2228224 | tf_op jit(solution)/shard_map/all_to_all | solution.py:439
  217.1 0.2 convert_reduce_fusion
  217.4 0.1 pad_maximum_fusion
  217.4 17.4 %all_to_all.49 = bf16[8,12,4,8,128]{4,3,2,1,0:T(8,128)(2,1)S(1)} all-to-all(bf16[8,12,4,8,128]{4,3,2,1,0:T(8,128)(2,1)S(1)} %pad_maximum_fusion), channel_id=1, replica_groups=mesh['yh'=4,'core'=2,'yl'=2,'x'=4,'z'=8] {'yl','x'}, dimensions={0} | all-to-all | bytes 1572864 | tf_op jit(solution)/shard_map/all_to_all | solution.py:439
  234.9 0.1 convert_reduce_fusion.1
  235.1 16.4 %all_to_all.50 = bf16[8,5,4,8,128]{4,3,2,1,0:T(8,128)(2,1)S(1)} all-to-all(bf16[8,5,4,8,128]{4,3,2,1,0:T(8,128)(2,1)S(1)} %pad_maximum_fusion.1), channel_id=1, replica_groups=mesh['yh'=4,'core'=2,'yl'=2,'x'=4,'z'=8] {'z'}, dimensions={0} | all-to-all | bytes 655360 | tf_op jit(solution)/shard_map/all_to_all | solution.py:439
  251.6 13.9 %all_to_all.51 = bf16[4,5,4,8,128]{4,3,2,1,0:T(8,128)(2,1)S(1)} all-to-all(bf16[4,5,4,8,128]{4,3,2,1,0:T(8,128)(2,1)S(1)} %broadcast_in_dim.22), channel_id=1, replica_groups=mesh['yh'=4,'core'=2,'yl'=2,'x'=4,'z'=8] {'yh'}, dimensions={0} | all-to-all | bytes 327680 | tf_op jit(solution)/shard_map/all_to_all | solution.py:439
  265.5 8.9 %all_to_all.52 = f32[2,5,4,8,128]{4,3,2,1,0:T(8,128)S(1)} all-to-all(f32[2,5,4,8,128]{4,3,2,1,0:T(8,128)S(1)} %broadcast_in_dim.23), channel_id=1, replica_groups=mesh['yh'=4,'core'=2,'yl'=2,'x'=4,'z'=8] {'core'}, dimensions={0} | all-to-all | bytes 327680 | tf_op jit(solution)/shard_map/all_to_all | solution.py:439
  274.4 0.7 copy.32
  275.0 0.6 slice.49
  (22 shorter events, 0.3 us)
Async XLA Ops:
  0.6 0.8 copy-start
  64.1 6.3 %copy-start.1 = (bf16[8,8,2,64,128]{4,3,2,1,0:T(8,128)(2,1)}, bf16[8,8,2,64,128]{4,3,2,1,0:T(8,128)(2,1)S(1)}, u32[]{:S(2)}) copy-start(bf16[8,8,2,64,128]{4,3,2,1,0:T(8,128)(2,1)S(1)} %all_to_all.46) | copy-start | bytes 6291460
  66.1 29.6 %all-to-all-start.1 = ((bf16[8,8,2,64,128]{4,3,2,1,0:T(8,128)(2,1)}), bf16[8,8,2,64,128]{4,3,2,1,0:T(8,128)(2,1)}, u32[]{:S(2)}, u32[]{:S(2)}) async-start(bf16[8,8,2,64,128]{4,3,2,1,0:T(8,128)(2,1)} %broadcast_in_dim.16), calls=%async_computation.1 | async-start | bytes 4194304 | tf_op jit(solution)/shard_map/all_to_all | solution.py:439
  70.5 111.8 %collective-permute-start = (bf16[2,32,4,32,128]{4,3,2,1,0:T(8,128)(2,1)S(1)}, bf16[2,32,4,32,128]{4,3,2,1,0:T(8,128)(2,1)}, u32[]{:S(2)}, u32[]{:S(2)}) collective-permute-start(bf16[2,32,4,32,128]{4,3,2,1,0:T(8,128)(2,1)S(1)} %bitcast.30), channel_id=1, source_target_pairs={{0,64},{64,0},{1,65},{65,1},{2,66},{66,2},{3,67},{67,3},{4,68},{68... | collective-permute-start | bytes 6291464 | tf_op jit(solution)/shard_map/ppermute | solution.py:463
  182.3 9.6 %copy-start.4 = (bf16[31,1024]{1,0:T(8,128)(2,1)S(1)}, bf16[31,1024]{1,0:T(8,128)(2,1)}, u32[]{:S(2)}) copy-start(bf16[31,1024]{1,0:T(8,128)(2,1)} %param.17) | copy-start | bytes 190468
  188.3 4.3 %collective-permute-start.1 = (bf16[48,1024]{1,0:T(8,128)(2,1)}, bf16[48,1024]{1,0:T(8,128)(2,1)S(1)}, u32[]{:S(2)}, u32[]{:S(2)}) collective-permute-start(bf16[48,1024]{1,0:T(8,128)(2,1)} %get-tuple-element.15), channel_id=1, source_target_pairs={{0,1},{1,2},{2,3},{3,4},{4,5},{5,6},{6,7},{7,8},{8,9},{9,10},{10,1... | collective-permute-start | bytes 294920 | tf_op jit(solution)/shard_map/ppermute | solution.py:470
  190.4 5.6 %collective-permute-start.2 = (bf16[48,1024]{1,0:T(8,128)(2,1)}, bf16[48,1024]{1,0:T(8,128)(2,1)S(1)}, u32[]{:S(2)}, u32[]{:S(2)}) collective-permute-start(bf16[48,1024]{1,0:T(8,128)(2,1)} %get-tuple-element.16), channel_id=1, source_target_pairs={{1,0},{2,1},{3,2},{4,3},{5,4},{6,5},{7,6},{8,7},{9,8},{10,9},{11,1... | collective-permute-start | bytes 294920 | tf_op jit(solution)/shard_map/ppermute | solution.py:471
  192.6 3.4 %copy-start.2 = (bf16[48,1024]{1,0:T(8,128)(2,1)}, bf16[48,1024]{1,0:T(8,128)(2,1)S(1)}, u32[]{:S(2)}) copy-start(bf16[48,1024]{1,0:T(8,128)(2,1)S(1)} %collective-permute-done.1.before_ref.cot_before_ref) | copy-start | bytes 294916
  196.0 0.6 copy-start.3

commit v3 on v2

--- a/solution.py
+++ b/solution.py
@@ -16,8 +16,9 @@
 F32 = jnp.float32
 BF16 = jnp.bfloat16
 
-YX = ("yl", "x")
-SEQ = ("yl", "x", "z")
+YX = ("yl", "xh", "xl")
+NEAR = ("yl", "xl")
+SEQ = ("yl", "xh", "xl", "z")
 NT = (((1,), (1,)), ((), ()))
 
 
@@ -153,15 +154,27 @@
         lax.fori_loop(0, sources, online, 0)
 
     done = (acc[0:64] / acc[64:65]).astype(BF16)
+    level = top[...] + jnp.log2(acc[64:65])
+    high = level.astype(BF16)
+    rest = level - high.astype(F32)
+    middle = rest.astype(BF16)
+    low = (rest - middle.astype(F32)).astype(BF16)
     for i in range(count):
-        o_ref[i] = done[:, i * 128 : i * 128 + 128]
+        cols = slice(i * 128, i * 128 + 128)
+        o_ref[i, 0:64] = done[:, cols]
+        row = lax.broadcasted_iota(jnp.int32, (16, 128), 0)
+        o_ref[i, 64:80] = jnp.where(
+            row == 0,
+            high[:, cols].astype(F32),
+            jnp.where(row == 1, middle[:, cols].astype(F32), low[:, cols].astype(F32)),
+        ).astype(BF16)
 
 
 def attend(q_t, kv):
     count = q_t.shape[0]
     return pl.pallas_call(
         attend_kernel,
-        out_shape=jax.ShapeDtypeStruct((count, 64, 128), BF16),
+        out_shape=jax.ShapeDtypeStruct((count, 80, 128), BF16),
         scratch_shapes=[
             pltpu.VMEM((256, count * 128), BF16),
             pltpu.VMEM((256, count * 128), BF16),
@@ -185,7 +198,8 @@
 
 def gate_kernel(
     core_ref, att_ref, out_proj_ref, residual_ref, gain_ref, cot_ref, own_ref, other_ref,
-    mid_ref, hat_ref, rscale_ref, value_ref, gate_ref, gated_ref, first_ref, last_ref, normed,
+    mid_ref, hat_ref, rscale_ref, value_ref, gate_ref, gated_ref, first_ref, last_ref, joined_ref,
+    normed,
 ):
     step = pl.program_id(0)
     core = core_ref[0]
@@ -193,7 +207,19 @@
 
     @pl.when(step == 0)
     def _():
-        att = att_ref[...].astype(F32).T.astype(BF16)
+        heads = []
+        for head in range(att_ref.shape[1]):
+            parts = [att_ref[side, head].astype(F32) for side in range(2)]
+            levels = [part[64:65] + part[65:66] + part[66:67] for part in parts]
+            highest = jnp.maximum(levels[0], levels[1])
+            shares = [jnp.exp2(level - highest) for level in levels]
+            heads.append(
+                (parts[0][0:64] * shares[0] + parts[1][0:64] * shares[1])
+                / (shares[0] + shares[1])
+            )
+        joined = jnp.concatenate(heads, axis=0)
+        joined_ref[...] = joined.astype(BF16)
+        att = joined.T.astype(BF16)
         mid = (
             residual_ref[...].astype(F32)
             + jnp.dot(att, out_proj_ref[...], preferred_element_type=F32)
@@ -258,6 +284,7 @@
             block(rows),
             block(48),
             block(48),
+            whole(HEADS * DH, rows),
         ],
         out_shape=[
             array((rows, model), BF16),
@@ -268,6 +295,7 @@
             array((rows, model), BF16),
             array((48, model), BF16),
             array((48, model), BF16),
+            array((HEADS * DH, rows), BF16),
         ],
         scratch_shapes=[pltpu.VMEM((2, rows, model // 2), BF16)],
         compiler_params=pltpu.CompilerParams(vmem_limit_bytes=56 * 1024 * 1024),
@@ -446,7 +474,6 @@
 def body(
     queries, keys, values, residual, out_proj, conv_in, conv_out, depth_kernel, norm_gain, cotangent
 ):
-    rows = queries.shape[1]
     model = residual.shape[2]
     core = lax.axis_index("core")
     place = core.astype(jnp.int32).reshape(1)
@@ -457,14 +484,20 @@
     share = lax.dynamic_slice_in_dim(conv_in, core * (model // 2), model // 2, axis=0)
     sent = pack(queries[0], keys[0], values[0], share)
     got = swap(sent, "z")
-    kv = spread(got[:, 1:3], YX, 8).reshape(64, 2, 64, 128)
+    mine = got[:, 0]
+    theirs = lax.ppermute(mine, "xh", [(0, 1), (1, 0)])
+    kv = spread(got[:, 1:3], NEAR, 4).reshape(32, 2, 64, 128)
+    upper = lax.axis_index("xh") == 1
+    query_blocks = jnp.concatenate(
+        [jnp.where(upper, theirs, mine), jnp.where(upper, mine, theirs)], axis=0
+    )
     own = spread(got[:, 3:5], YX, 8).reshape(2, 32, 4, 32, 128)
-    attended = attend(got[:, 0], kv)
+    attended = attend(query_blocks, kv)
     other = lax.ppermute(own, "core", [(0, 1), (1, 0)])
-    att = swap(attended, "z").reshape(HEADS * DH, rows)
-
-    mid, hat, rscale, value_half, gate_half, gated, first, last = gate(
-        place, att, out_proj, residual[0], gain, cot, own, other
+    parts = swap(attended, ("xh", "z")).reshape(2, HEADS, 80, 128)
+
+    mid, hat, rscale, value_half, gate_half, gated, first, last, att = gate(
+        place, parts, out_proj, residual[0], gain, cot, own, other
     )
     count = 64
     before = lax.ppermute(last, SEQ, [(i, i + 1) for i in range(count - 1)])
@@ -492,7 +525,7 @@
 
 
 def solution(mesh):
-    split = Mesh(mesh.devices.reshape(4, 2, 2, 4, 8), ("yh", "core", "yl", "x", "z"))
+    split = Mesh(mesh.devices.reshape(4, 2, 2, 2, 2, 8), ("yh", "core", "yl", "xh", "xl", "z"))
     rows = P(("yh", "core"), SEQ, None)
     return jax.shard_map(
         body,

time: 276 us -> 269 us (0.975)
  waiting for transfers between devices: 22.3 us -> 16.2 us
  Pallas kernels: 93.4 us -> 88.5 us
  blocking collectives: 137 us -> 140 us
    all_to_all x1, waiting for transfers between devices: 18.8 us -> 0.01 us  [swap(): return lax.all_to_all(array, axes, split_axis=0, concat_axis=0, tiled=True)]
    ppermute x0 -> x1, waiting for transfers between devices: none -> 12.3 us  [body(): theirs = lax.ppermute(mine, 'xh', [(0, 1), (1, 0)])]
    pallas_call x1, Pallas kernels: 74.2 us -> 69.2 us  [attend(): pl.pallas_call(attend_kernel, out_shape=jax.ShapeDtypeStruct((count, 80,...]
    ppermute x0 -> x1, starting transfers between devices: none -> 3.15 us  [body(): theirs = lax.ppermute(mine, 'xh', [(0, 1), (1, 0)])]
  transfers between devices with their start and end apart: 4 -> 5, of which waited for: 2 -> 3; matrix products, arithmetic and copies ran while one was open for 0% -> 1% of each run, Pallas kernels for 27% -> 26%
where the time goes in v3:
time: 269 us; the launch traced here: 268 us
  blocking collectives  140 us (52%)
  Pallas kernels  88.5 us (33%)
  waiting for transfers between devices  16.2 us (6%)
  starting transfers between devices  15.4 us (6%)
  local copies, waits for them, and re-layouts  5.67 us (2%)
    all_to_all x8, blocking collectives, swap(): return lax.all_to_all(array, axes, split_axis=0, concat_axis=0, tiled=True)  140 us
    pallas_call x1, Pallas kernels, attend(): pl.pallas_call(attend_kernel, out_shape=jax.ShapeDtypeStruct((count, 80,...  69.2 us
    ppermute x1, waiting for transfers between devices, body(): theirs = lax.ppermute(mine, 'xh', [(0, 1), (1, 0)])  12.3 us
    pallas_call x1, Pallas kernels, back(): pl.pallas_call(back_kernel, grid=(STEPS,), in_specs=[pl.BlockSpec(memory_...  11.1 us
    pallas_call x1, Pallas kernels, gate(): pl.pallas_call(gate_kernel, grid=(STEPS,), in_specs=[pl.BlockSpec(memory_...  6.13 us
  transfers between devices with their start and end apart: 5, of which 3 were waited for; matrix products, arithmetic and copies ran while one was open for 1% of the time, Pallas kernels for 26%

profile of v3, /device:TPU:1, one launch (start us, length us, event | category | flops | bytes accessed | tf_op | source)
XLA Modules:
  0.0 268.3 jit_solution(2079380355989879775)
XLA Ops:
  0.7 0.8 copy-done
  1.5 0.8 copy.30.w_ref
  2.2 2.1 shard_map.129
  4.4 30.1 %all_to_all.45 = bf16[8,5,64,128]{3,2,1,0:T(8,128)(2,1)S(1)} all-to-all(bf16[8,5,64,128]{3,2,1,0:T(8,128)(2,1)} %shard_map.129), channel_id=1, replica_groups=mesh['yh'=4,'core'=2,'yl'=2,'xh'=2,'xl'=2,'z'=8] {'z'}, dimensions={0} | all-to-all | bytes 1310720 | tf_op jit(solution)/shard_map/all_to_all | solution.py:467
  34.5 0.5 broadcast_in_dim.17
  35.0 29.1 %all_to_all.46 = bf16[8,8,2,64,128]{4,3,2,1,0:T(8,128)(2,1)S(1)} all-to-all(bf16[8,8,2,64,128]{4,3,2,1,0:T(8,128)(2,1)S(1)} %broadcast_in_dim.17), channel_id=1, replica_groups=mesh['yh'=4,'core'=2,'yl'=2,'xh'=2,'xl'=2,'z'=8] {'yl','xh','xl'}, dimensions={0} | all-to-all | bytes 4194304 | tf_op jit(solution)/shard_map/all_to_all | solution.py:467
  64.1 1.4 broadcast_in_dim.16
  65.6 4.2 %all-to-all-start.1 = ((bf16[4,8,2,64,128]{4,3,2,1,0:T(8,128)(2,1)}), bf16[4,8,2,64,128]{4,3,2,1,0:T(8,128)(2,1)}, u32[]{:S(2)}, u32[]{:S(2)}) async-start(bf16[4,8,2,64,128]{4,3,2,1,0:T(8,128)(2,1)} %broadcast_in_dim.16), calls=%async_computation.1 | async-start | bytes 2097152 | tf_op jit(solution)/shard_map/all_to_all | solution.py:467
  69.8 3.1 %collective-permute-start = (bf16[8,64,128]{2,1,0:T(8,128)(2,1)S(1)}, bf16[8,64,128]{2,1,0:T(8,128)(2,1)S(1)}, u32[]{:S(2)}, u32[]{:S(2)}) collective-permute-start(bf16[8,64,128]{2,1,0:T(8,128)(2,1)S(1)} %slice_bitcast_fusion), channel_id=1, source_target_pairs={{0,16},{16,0},{1,17},{17,1},{2,18},{18,2},{3,19},{19,3},{4,20},{20... | collective-permute-start | bytes 393224 | tf_op jit(solution)/shard_map/ppermute | solution.py:488
  73.0 12.3 %collective-permute-done = bf16[8,64,128]{2,1,0:T(8,128)(2,1)S(1)} collective-permute-done((bf16[8,64,128]{2,1,0:T(8,128)(2,1)S(1)}, bf16[8,64,128]{2,1,0:T(8,128)(2,1)S(1)}, u32[]{:S(2)}, u32[]{:S(2)}) %collective-permute-start) | collective-permute-done | bytes 131104 | tf_op jit(solution)/shard_map/ppermute | solution.py:488
  85.3 0.7 pad_maximum_fusion.2.q_ref
  86.0 3.6 %collective-permute-start.1 = (bf16[2,32,4,32,128]{4,3,2,1,0:T(8,128)(2,1)S(1)}, bf16[2,32,4,32,128]{4,3,2,1,0:T(8,128)(2,1)}, u32[]{:S(2)}, u32[]{:S(2)}) collective-permute-start(bf16[2,32,4,32,128]{4,3,2,1,0:T(8,128)(2,1)S(1)} %bitcast.34), channel_id=1, source_target_pairs={{0,64},{64,0},{1,65},{65,1},{2,66},{66,2},{3,67},{67,3},{4,68},{68... | collective-permute-start | bytes 6291464 | tf_op jit(solution)/shard_map/ppermute | solution.py:496
  89.6 69.2 %shard_map.130 = bf16[16,80,128]{2,1,0:T(8,128)(2,1)} custom-call(bf16[16,64,128]{2,1,0:T(8,128)(2,1)} %pad_maximum_fusion.2.q_ref, bf16[32,2,64,128]{3,2,1,0:T(8,128)(2,1)} %bitcast.5.kv_ref), custom_call_target="tpu_custom_call" | custom-call | flops 17179869184 | bytes 2097152 | tf_op jit(solution)/shard_map/pallas_call | solution.py:175
  158.8 17.7 %all_to_all.47 = bf16[16,80,128]{2,1,0:T(8,128)(2,1)} all-to-all(bf16[16,80,128]{2,1,0:T(8,128)(2,1)} %shard_map.130), channel_id=1, replica_groups=mesh['yh'=4,'core'=2,'yl'=2,'xh'=2,'xl'=2,'z'=8] {'xh','z'}, dimensions={0} | all-to-all | bytes 655360 | tf_op jit(solution)/shard_map/all_to_all | solution.py:467
  176.5 6.1 %shard_map.131 = (bf16[128,1024]{1,0:T(8,128)(2,1)}, f32[128,1024]{1,0:T(8,128)}, f32[128,128]{1,0:T(8,128)}, f32[128,1024]{1,0:T(8,128)}, f32[128,1024]{1,0:T(8...) custom-call(s32[1]{0:T(128)} %bitcast.core_ref, ...), custom_call_target="tpu_custom_call" | custom-call | tf_op jit(solution)/shard_map/pallas_call | solution.py:265
  182.6 3.0 %collective-permute-start.2 = (bf16[48,1024]{1,0:T(8,128)(2,1)}, bf16[48,1024]{1,0:T(8,128)(2,1)S(1)}, u32[]{:S(2)}, u32[]{:S(2)}) collective-permute-start(bf16[48,1024]{1,0:T(8,128)(2,1)} %get-tuple-element.16), channel_id=1, source_target_pairs={{0,1},{1,2},{2,3},{3,4},{4,5},{5,6},{6,7},{7,8},{8,9},{9,10},{10,1... | collective-permute-start | bytes 294920 | tf_op jit(solution)/shard_map/ppermute | solution.py:503
  185.6 1.5 collective-permute-start.3
  187.1 0.7 pad_convert_fusion.taps_ref
  187.7 0.2 collective-permute-done.2.before_ref.cot_before_ref
  187.9 3.7 %collective-permute-done.3.after_ref.cot_after_ref = bf16[48,1024]{1,0:T(8,128)(2,1)S(1)} collective-permute-done((bf16[48,1024]{1,0:T(8,128)(2,1)}, bf16[48,1024]{1,0:T(8,128)(2,1)S(1)}, u32[]{:S(2)}, u32[]{:S(2)}) %collective-permute-start.3) | collective-permute-done | bytes 98336 | tf_op jit(solution)/shard_map/ppermute | solution.py:504
  191.7 0.6 copy-done.3
  192.3 11.1 %shard_map.132 = (bf16[128,1024]{1,0:T(8,128)(2,1)}, bf16[128,1024]{1,0:T(8,128)(2,1)}, bf16[2,68,4,8,128]{4,3,2,1,0:T(8,128)(2,1)}) custom-call(s32[1]{0:T(128)} %bitcast.core_ref, bf16[48,1024]{1,0:T(8,128)(2,1)} %copy-done.2, bf16[48,1024]{1,0:T(8,128)(2,1)} %copy-done.3, bf16[128,1024]{1,0:T(8,128)(2,1)} %get-tuple-element.18.gated_ref, ...), custom_call_target="tpu_custom_call" | custom-call | tf_op jit(solution)/shard_map/pallas_call | solution.py:421
  203.4 6.6 %all_to_all.48 = bf16[2,68,4,8,128]{4,3,2,1,0:T(8,128)(2,1)S(1)} all-to-all(bf16[2,68,4,8,128]{4,3,2,1,0:T(8,128)(2,1)} %get-tuple-element.27), channel_id=1, replica_groups=mesh['yh'=4,'core'=2,'yl'=2,'xh'=2,'xl'=2,'z'=8] {'core'}, dimensions={0} | all-to-all | bytes 2228224 | tf_op jit(solution)/shard_map/all_to_all | solution.py:467
  210.0 0.2 convert_reduce_fusion
  210.3 0.1 pad_maximum_fusion
  210.4 17.0 %all_to_all.49 = bf16[8,12,4,8,128]{4,3,2,1,0:T(8,128)(2,1)S(1)} all-to-all(bf16[8,12,4,8,128]{4,3,2,1,0:T(8,128)(2,1)S(1)} %pad_maximum_fusion), channel_id=1, replica_groups=mesh['yh'=4,'core'=2,'yl'=2,'xh'=2,'xl'=2,'z'=8] {'yl','xh','xl'}, dimensions={0} | all-to-all | bytes 1572864 | tf_op jit(solution)/shard_map/all_to_all | solution.py:467
  227.4 0.1 convert_reduce_fusion.1
  227.6 15.9 %all_to_all.50 = bf16[8,5,4,8,128]{4,3,2,1,0:T(8,128)(2,1)S(1)} all-to-all(bf16[8,5,4,8,128]{4,3,2,1,0:T(8,128)(2,1)S(1)} %pad_maximum_fusion.1), channel_id=1, replica_groups=mesh['yh'=4,'core'=2,'yl'=2,'xh'=2,'xl'=2,'z'=8] {'z'}, dimensions={0} | all-to-all | bytes 655360 | tf_op jit(solution)/shard_map/all_to_all | solution.py:467
  243.6 14.5 %all_to_all.51 = bf16[4,5,4,8,128]{4,3,2,1,0:T(8,128)(2,1)S(1)} all-to-all(bf16[4,5,4,8,128]{4,3,2,1,0:T(8,128)(2,1)S(1)} %broadcast_in_dim.22), channel_id=1, replica_groups=mesh['yh'=4,'core'=2,'yl'=2,'xh'=2,'xl'=2,'z'=8] {'yh'}, dimensions={0} | all-to-all | bytes 327680 | tf_op jit(solution)/shard_map/all_to_all | solution.py:467
  258.1 8.9 %all_to_all.52 = f32[2,5,4,8,128]{4,3,2,1,0:T(8,128)S(1)} all-to-all(f32[2,5,4,8,128]{4,3,2,1,0:T(8,128)S(1)} %broadcast_in_dim.23), channel_id=1, replica_groups=mesh['yh'=4,'core'=2,'yl'=2,'xh'=2,'xl'=2,'z'=8] {'core'}, dimensions={0} | all-to-all | bytes 327680 | tf_op jit(solution)/shard_map/all_to_all | solution.py:467
  267.0 0.7 copy.32
  267.7 0.6 slice.49
  (26 shorter events, 0.4 us)
Async XLA Ops:
  0.6 0.8 copy-start
  64.1 21.9 %copy-start.1 = (bf16[8,8,2,64,128]{4,3,2,1,0:T(8,128)(2,1)}, bf16[8,8,2,64,128]{4,3,2,1,0:T(8,128)(2,1)S(1)}, u32[]{:S(2)}) copy-start(bf16[8,8,2,64,128]{4,3,2,1,0:T(8,128)(2,1)S(1)} %all_to_all.46) | copy-start | bytes 6291460
  65.6 24.0 %all-to-all-start.1 = ((bf16[4,8,2,64,128]{4,3,2,1,0:T(8,128)(2,1)}), bf16[4,8,2,64,128]{4,3,2,1,0:T(8,128)(2,1)}, u32[]{:S(2)}, u32[]{:S(2)}) async-start(bf16[4,8,2,64,128]{4,3,2,1,0:T(8,128)(2,1)} %broadcast_in_dim.16), calls=%async_computation.1 | async-start | bytes 2097152 | tf_op jit(solution)/shard_map/all_to_all | solution.py:467
  69.8 15.4 %collective-permute-start = (bf16[8,64,128]{2,1,0:T(8,128)(2,1)S(1)}, bf16[8,64,128]{2,1,0:T(8,128)(2,1)S(1)}, u32[]{:S(2)}, u32[]{:S(2)}) collective-permute-start(bf16[8,64,128]{2,1,0:T(8,128)(2,1)S(1)} %slice_bitcast_fusion), channel_id=1, source_target_pairs={{0,16},{16,0},{1,17},{17,1},{2,18},{18,2},{3,19},{19,3},{4,20},{20... | collective-permute-start | bytes 393224 | tf_op jit(solution)/shard_map/ppermute | solution.py:488
  86.0 90.5 %collective-permute-start.1 = (bf16[2,32,4,32,128]{4,3,2,1,0:T(8,128)(2,1)S(1)}, bf16[2,32,4,32,128]{4,3,2,1,0:T(8,128)(2,1)}, u32[]{:S(2)}, u32[]{:S(2)}) collective-permute-start(bf16[2,32,4,32,128]{4,3,2,1,0:T(8,128)(2,1)S(1)} %bitcast.34), channel_id=1, source_target_pairs={{0,64},{64,0},{1,65},{65,1},{2,66},{66,2},{3,67},{67,3},{4,68},{68... | collective-permute-start | bytes 6291464 | tf_op jit(solution)/shard_map/ppermute | solution.py:496
  176.5 10.6 %copy-start.4 = (bf16[31,1024]{1,0:T(8,128)(2,1)S(1)}, bf16[31,1024]{1,0:T(8,128)(2,1)}, u32[]{:S(2)}) copy-start(bf16[31,1024]{1,0:T(8,128)(2,1)} %param.17) | copy-start | bytes 190468
  182.6 5.4 %collective-permute-start.2 = (bf16[48,1024]{1,0:T(8,128)(2,1)}, bf16[48,1024]{1,0:T(8,128)(2,1)S(1)}, u32[]{:S(2)}, u32[]{:S(2)}) collective-permute-start(bf16[48,1024]{1,0:T(8,128)(2,1)} %get-tuple-element.16), channel_id=1, source_target_pairs={{0,1},{1,2},{2,3},{3,4},{4,5},{5,6},{6,7},{7,8},{8,9},{9,10},{10,1... | collective-permute-start | bytes 294920 | tf_op jit(solution)/shard_map/ppermute | solution.py:503
  185.6 6.1 %collective-permute-start.3 = (bf16[48,1024]{1,0:T(8,128)(2,1)}, bf16[48,1024]{1,0:T(8,128)(2,1)S(1)}, u32[]{:S(2)}, u32[]{:S(2)}) collective-permute-start(bf16[48,1024]{1,0:T(8,128)(2,1)} %get-tuple-element.17), channel_id=1, source_target_pairs={{1,0},{2,1},{3,2},{4,3},{5,4},{6,5},{7,6},{8,7},{9,8},{10,9},{11,1... | collective-permute-start | bytes 294920 | tf_op jit(solution)/shard_map/ppermute | solution.py:504
  187.9 3.7 %copy-start.2 = (bf16[48,1024]{1,0:T(8,128)(2,1)}, bf16[48,1024]{1,0:T(8,128)(2,1)S(1)}, u32[]{:S(2)}) copy-start(bf16[48,1024]{1,0:T(8,128)(2,1)S(1)} %collective-permute-done.2.before_ref.cot_before_ref) | copy-start | bytes 294916
  191.7 0.6 copy-start.3

commit v4 on v3

--- a/solution.py
+++ b/solution.py
@@ -22,7 +22,7 @@
 NT = (((1,), (1,)), ((), ()))
 
 
-def pack_kernel(q_ref, k_ref, v_ref, w_ref, o_ref):
+def pack_kernel(core_ref, q_ref, k_ref, v_ref, w_ref, o_ref):
     for pair in range(HEADS // 2):
         cols = pl.ds(pair * 128, 128)
         q_t = q_ref[:, cols].astype(F32).T.astype(BF16)
@@ -37,23 +37,24 @@
             o_ref[head, 0] = q_t[half * 64 : half * 64 + 64]
             o_ref[head, 1] = packed
             o_ref[head, 2] = v_t[half * 64 : half * 64 + 64]
+    features = w_ref.shape[1] // 2
+    share = jnp.where(
+        core_ref[0] == 0, w_ref[:, :features].astype(F32), w_ref[:, features:].astype(F32)
+    ).astype(BF16)
     for half in range(2):
-        turned = jnp.concatenate(
-            [
-                w_ref[half * 256 + b * 128 : half * 256 + b * 128 + 128, :].astype(F32).T
-                for b in range(2)
-            ],
-            axis=0,
-        ).astype(BF16)
+        blocks = [share[:, (2 * half + b) * 128 : (2 * half + b + 1) * 128] for b in range(2)]
         for head in range(HEADS):
-            o_ref[head, 3 + half] = turned
-
-
-def pack(q, k, v, w):
+            o_ref[head, 3 + half] = jnp.concatenate(blocks, axis=0)
+
+
+def pack(core, q, k, v, w):
+    local = pl.BlockSpec(memory_space=pltpu.VMEM)
     return pl.pallas_call(
         pack_kernel,
+        in_specs=[pl.BlockSpec(memory_space=pltpu.SMEM), local, local, local, local],
         out_shape=jax.ShapeDtypeStruct((HEADS, 5, 64, 128), BF16),
-    )(q, k, v, w)
+        compiler_params=pltpu.CompilerParams(vmem_limit_bytes=56 * 1024 * 1024),
+    )(core, q, k, v, w)
 
 
 SCALE = DH ** (-0.5) * math.log2(math.e)
@@ -182,7 +183,7 @@
             pltpu.VMEM((80, count * 128), F32),
         ],
         cost_estimate=COST,
-        compiler_params=pltpu.CompilerParams(vmem_limit_bytes=56 * 1024 * 1024),
+        compiler_params=pltpu.CompilerParams(vmem_limit_bytes=24 * 1024 * 1024),
     )(q_t, kv)
 
 
@@ -298,7 +299,7 @@
             array((HEADS * DH, rows), BF16),
         ],
         scratch_shapes=[pltpu.VMEM((2, rows, model // 2), BF16)],
-        compiler_params=pltpu.CompilerParams(vmem_limit_bytes=56 * 1024 * 1024),
+        compiler_params=pltpu.CompilerParams(vmem_limit_bytes=16 * 1024 * 1024),
     )(core, att, out_proj, residual, gain, cot, own, other)
 
 
@@ -458,7 +459,7 @@
             pltpu.VMEM((rows, model), F32),
             pltpu.VMEM((2, rows, model // 2), F32),
         ],
-        compiler_params=pltpu.CompilerParams(vmem_limit_bytes=56 * 1024 * 1024),
+        compiler_params=pltpu.CompilerParams(vmem_limit_bytes=20 * 1024 * 1024),
     )(core, before, after, gated, before, after, cot, conv_out, taps, value, gate_half, own, other,
       mid, hat, rscale, gain, att)
 
@@ -481,8 +482,7 @@
     cot = cotangent[0]
     taps = jnp.pad(depth_kernel.astype(F32), ((0, 1), (0, 0)))
 
-    share = lax.dynamic_slice_in_dim(conv_in, core * (model // 2), model // 2, axis=0)
-    sent = pack(queries[0], keys[0], values[0], share)
+    sent = pack(place, queries[0], keys[0], values[0], conv_in.T)
     got = swap(sent, "z")
     mine = got[:, 0]
     theirs = lax.ppermute(mine, "xh", [(0, 1), (1, 0)])

time: 269 us -> 261 us (0.970)
  Pallas kernels: 88.5 us -> 83.8 us
  blocking collectives: 140 us -> 137 us
where the time goes in v4:
time: 261 us; the launch traced here: 260 us
  blocking collectives  137 us (52%)
  Pallas kernels  83.8 us (32%)
  waiting for transfers between devices  16.3 us (6%)
  starting transfers between devices  15.1 us (6%)
  local copies, waits for them, and re-layouts  5 us (2%)
    all_to_all x8, blocking collectives, swap(): return lax.all_to_all(array, axes, split_axis=0, concat_axis=0, tiled=True)  137 us
    pallas_call x1, Pallas kernels, attend(): pl.pallas_call(attend_kernel, out_shape=jax.ShapeDtypeStruct((count, 80,...  67.1 us
    ppermute x1, waiting for transfers between devices, body(): theirs = lax.ppermute(mine, 'xh', [(0, 1), (1, 0)])  11.4 us
    pallas_call x1, Pallas kernels, back(): pl.pallas_call(back_kernel, grid=(STEPS,), in_specs=[pl.BlockSpec(memory_...  9.93 us
  transfers between devices with their start and end apart: 5, of which 3 were waited for; matrix products, arithmetic and copies ran while one was open for 1% of the time, Pallas kernels for 26%

profile of v4, /device:TPU:1, one launch (start us, length us, event | category | flops | bytes accessed | tf_op | source)
XLA Modules:
  0.0 259.9 jit_solution(10665812344563033085)
XLA Ops:
  0.6 2.1 shard_map.129
  2.7 30.1 %all_to_all.45 = bf16[8,5,64,128]{3,2,1,0:T(8,128)(2,1)S(1)} all-to-all(bf16[8,5,64,128]{3,2,1,0:T(8,128)(2,1)} %shard_map.129), channel_id=1, replica_groups=mesh['yh'=4,'core'=2,'yl'=2,'xh'=2,'xl'=2,'z'=8] {'z'}, dimensions={0} | all-to-all | bytes 1310720 | tf_op jit(solution)/shard_map/all_to_all | solution.py:468
  32.8 0.8 copy-done.5
  33.6 0.5 broadcast_in_dim.17
  34.1 29.1 %all_to_all.46 = bf16[8,8,2,64,128]{4,3,2,1,0:T(8,128)(2,1)S(1)} all-to-all(bf16[8,8,2,64,128]{4,3,2,1,0:T(8,128)(2,1)S(1)} %broadcast_in_dim.17), channel_id=1, replica_groups=mesh['yh'=4,'core'=2,'yl'=2,'xh'=2,'xl'=2,'z'=8] {'yl','xh','xl'}, dimensions={0} | all-to-all | bytes 4194304 | tf_op jit(solution)/shard_map/all_to_all | solution.py:468
  63.3 1.2 broadcast_in_dim.16
  64.5 3.5 %all-to-all-start.1 = ((bf16[4,8,2,64,128]{4,3,2,1,0:T(8,128)(2,1)}), bf16[4,8,2,64,128]{4,3,2,1,0:T(8,128)(2,1)S(1)}, u32[]{:S(2)}, u32[]{:S(2)}) async-start(bf16[4,8,2,64,128]{4,3,2,1,0:T(8,128)(2,1)} %broadcast_in_dim.16), calls=%async_computation.1 | async-start | bytes 2097152 | tf_op jit(solution)/shard_map/all_to_all | solution.py:468
  68.0 0.9 slice_bitcast_fusion
  69.0 3.1 %collective-permute-start = (bf16[8,64,128]{2,1,0:T(8,128)(2,1)S(1)}, bf16[8,64,128]{2,1,0:T(8,128)(2,1)S(1)}, u32[]{:S(2)}, u32[]{:S(2)}) collective-permute-start(bf16[8,64,128]{2,1,0:T(8,128)(2,1)S(1)} %slice_bitcast_fusion), channel_id=1, source_target_pairs={{0,16},{16,0},{1,17},{17,1},{2,18},{18,2},{3,19},{19,3},{4,20},{20... | collective-permute-start | bytes 393224 | tf_op jit(solution)/shard_map/ppermute | solution.py:488
  72.1 11.4 %collective-permute-done = bf16[8,64,128]{2,1,0:T(8,128)(2,1)S(1)} collective-permute-done((bf16[8,64,128]{2,1,0:T(8,128)(2,1)S(1)}, bf16[8,64,128]{2,1,0:T(8,128)(2,1)S(1)}, u32[]{:S(2)}, u32[]{:S(2)}) %collective-permute-start) | collective-permute-done | bytes 131104 | tf_op jit(solution)/shard_map/ppermute | solution.py:488
  83.5 0.9 broadcast_select_fusion.1
  84.4 3.6 %collective-permute-start.1 = (bf16[2,32,4,32,128]{4,3,2,1,0:T(8,128)(2,1)S(1)}, bf16[2,32,4,32,128]{4,3,2,1,0:T(8,128)(2,1)}, u32[]{:S(2)}, u32[]{:S(2)}) collective-permute-start(bf16[2,32,4,32,128]{4,3,2,1,0:T(8,128)(2,1)S(1)} %bitcast.35), channel_id=1, source_target_pairs={{0,64},{64,0},{1,65},{65,1},{2,66},{66,2},{3,67},{67,3},{4,68},{68... | collective-permute-start | bytes 6291464 | tf_op jit(solution)/shard_map/ppermute | solution.py:496
  88.0 0.0 copy-start.1
  88.0 0.0 copy-start.2
  88.1 67.1 %shard_map.130 = bf16[16,80,128]{2,1,0:T(8,128)(2,1)S(1)} custom-call(bf16[16,64,128]{2,1,0:T(8,128)(2,1)S(1)} %pad_maximum_fusion.2.q_ref, bf16[32,2,64,128]{3,2,1,0:T(8,128)(2,1)S(1)} %bitcast.41), custom_call_target="tpu_custom_call" | custom-call | flops 17179869184 | bytes 2097152 | tf_op jit(solution)/shard_map/pallas_call | solution.py:176
  155.2 16.9 %all_to_all.47 = bf16[16,80,128]{2,1,0:T(8,128)(2,1)S(1)} all-to-all(bf16[16,80,128]{2,1,0:T(8,128)(2,1)S(1)} %shard_map.130), channel_id=1, replica_groups=mesh['yh'=4,'core'=2,'yl'=2,'xh'=2,'xl'=2,'z'=8] {'xh','z'}, dimensions={0} | all-to-all | bytes 655360 | tf_op jit(solution)/shard_map/all_to_all | solution.py:468
  172.2 4.7 %shard_map.131 = (bf16[128,1024]{1,0:T(8,128)(2,1)S(1)}, f32[128,1024]{1,0:T(8,128)S(1)}, f32[128,128]{1,0:T(8,128)S(1)}, f32[128,1024]{1,0:T(8,128)S(1)}, f32[1...) custom-call(s32[1]{0:T(128)} %bitcast.core_ref, ...), custom_call_target="tpu_custom_call" | custom-call | tf_op jit(solution)/shard_map/pallas_call | solution.py:266
  176.9 3.4 %collective-permute-start.2 = (bf16[48,1024]{1,0:T(8,128)(2,1)S(1)}, bf16[48,1024]{1,0:T(8,128)(2,1)S(1)}, u32[]{:S(2)}, u32[]{:S(2)}) collective-permute-start(bf16[48,1024]{1,0:T(8,128)(2,1)S(1)} %get-tuple-element.16), channel_id=1, source_target_pairs={{0,1},{1,2},{2,3},{3,4},{4,5},{5,6},{6,7},{7,8},{8,9},{9,10},{10,1... | collective-permute-start | bytes 294920 | tf_op jit(solution)/shard_map/ppermute | solution.py:503
  180.3 1.5 collective-permute-start.3
  181.8 1.1 collective-permute-done.2.before_ref.cot_before_ref
  182.9 3.9 %collective-permute-done.3.after_ref.cot_after_ref = bf16[48,1024]{1,0:T(8,128)(2,1)S(1)} collective-permute-done((bf16[48,1024]{1,0:T(8,128)(2,1)S(1)}, bf16[48,1024]{1,0:T(8,128)(2,1)S(1)}, u32[]{:S(2)}, u32[]{:S(2)}) %collective-permute-start.3) | collective-permute-done | bytes 98336 | tf_op jit(solution)/shard_map/ppermute | solution.py:504
  186.8 9.9 %shard_map.132 = (bf16[128,1024]{1,0:T(8,128)(2,1)}, bf16[128,1024]{1,0:T(8,128)(2,1)}, bf16[2,68,4,8,128]{4,3,2,1,0:T(8,128)(2,1)S(1)}) custom-call(s32[1]{0:T(128)} %bitcast.core_ref, bf16[48,1024]{1,0:T(8,128)(2,1)S(1)} %collective-permute-done.2.before_ref.cot_before_ref, bf16[48,1024]{1,0:T(8,128)(2,1)S(1)} %collective-permute-done.3.after_ref.cot_after_ref, ...), custom_call_target="tpu_custom_call" | custom-call | tf_op jit(solution)/shard_map/pallas_call | solution.py:422
  196.7 4.9 %all_to_all.48 = bf16[2,68,4,8,128]{4,3,2,1,0:T(8,128)(2,1)S(1)} all-to-all(bf16[2,68,4,8,128]{4,3,2,1,0:T(8,128)(2,1)S(1)} %get-tuple-element.27), channel_id=1, replica_groups=mesh['yh'=4,'core'=2,'yl'=2,'xh'=2,'xl'=2,'z'=8] {'core'}, dimensions={0} | all-to-all | bytes 2228224 | tf_op jit(solution)/shard_map/all_to_all | solution.py:468
  201.6 0.2 convert_reduce_fusion
  201.9 0.1 pad_maximum_fusion
  201.9 17.1 %all_to_all.49 = bf16[8,12,4,8,128]{4,3,2,1,0:T(8,128)(2,1)S(1)} all-to-all(bf16[8,12,4,8,128]{4,3,2,1,0:T(8,128)(2,1)S(1)} %pad_maximum_fusion), channel_id=1, replica_groups=mesh['yh'=4,'core'=2,'yl'=2,'xh'=2,'xl'=2,'z'=8] {'yl','xh','xl'}, dimensions={0} | all-to-all | bytes 1572864 | tf_op jit(solution)/shard_map/all_to_all | solution.py:468
  219.0 0.1 convert_reduce_fusion.1
  219.3 15.4 %all_to_all.50 = bf16[8,5,4,8,128]{4,3,2,1,0:T(8,128)(2,1)S(1)} all-to-all(bf16[8,5,4,8,128]{4,3,2,1,0:T(8,128)(2,1)S(1)} %pad_maximum_fusion.1), channel_id=1, replica_groups=mesh['yh'=4,'core'=2,'yl'=2,'xh'=2,'xl'=2,'z'=8] {'z'}, dimensions={0} | all-to-all | bytes 655360 | tf_op jit(solution)/shard_map/all_to_all | solution.py:468
  234.7 15.0 %all_to_all.51 = bf16[4,5,4,8,128]{4,3,2,1,0:T(8,128)(2,1)S(1)} all-to-all(bf16[4,5,4,8,128]{4,3,2,1,0:T(8,128)(2,1)S(1)} %broadcast_in_dim.22), channel_id=1, replica_groups=mesh['yh'=4,'core'=2,'yl'=2,'xh'=2,'xl'=2,'z'=8] {'yh'}, dimensions={0} | all-to-all | bytes 327680 | tf_op jit(solution)/shard_map/all_to_all | solution.py:468
  249.7 8.9 %all_to_all.52 = f32[2,5,4,8,128]{4,3,2,1,0:T(8,128)S(1)} all-to-all(f32[2,5,4,8,128]{4,3,2,1,0:T(8,128)S(1)} %broadcast_in_dim.23), channel_id=1, replica_groups=mesh['yh'=4,'core'=2,'yl'=2,'xh'=2,'xl'=2,'z'=8] {'core'}, dimensions={0} | all-to-all | bytes 327680 | tf_op jit(solution)/shard_map/all_to_all | solution.py:468
  258.6 0.7 copy.27
  259.3 0.6 slice.49
  (28 shorter events, 0.4 us)
Async XLA Ops:
  32.8 0.8 copy-start.5
  64.5 23.5 %all-to-all-start.1 = ((bf16[4,8,2,64,128]{4,3,2,1,0:T(8,128)(2,1)}), bf16[4,8,2,64,128]{4,3,2,1,0:T(8,128)(2,1)S(1)}, u32[]{:S(2)}, u32[]{:S(2)}) async-start(bf16[4,8,2,64,128]{4,3,2,1,0:T(8,128)(2,1)} %broadcast_in_dim.16), calls=%async_computation.1 | async-start | bytes 2097152 | tf_op jit(solution)/shard_map/all_to_all | solution.py:468
  69.0 14.5 %collective-permute-start = (bf16[8,64,128]{2,1,0:T(8,128)(2,1)S(1)}, bf16[8,64,128]{2,1,0:T(8,128)(2,1)S(1)}, u32[]{:S(2)}, u32[]{:S(2)}) collective-permute-start(bf16[8,64,128]{2,1,0:T(8,128)(2,1)S(1)} %slice_bitcast_fusion), channel_id=1, source_target_pairs={{0,16},{16,0},{1,17},{17,1},{2,18},{18,2},{3,19},{19,3},{4,20},{20... | collective-permute-start | bytes 393224 | tf_op jit(solution)/shard_map/ppermute | solution.py:488
  84.4 87.7 %collective-permute-start.1 = (bf16[2,32,4,32,128]{4,3,2,1,0:T(8,128)(2,1)S(1)}, bf16[2,32,4,32,128]{4,3,2,1,0:T(8,128)(2,1)}, u32[]{:S(2)}, u32[]{:S(2)}) collective-permute-start(bf16[2,32,4,32,128]{4,3,2,1,0:T(8,128)(2,1)S(1)} %bitcast.35), channel_id=1, source_target_pairs={{0,64},{64,0},{1,65},{65,1},{2,66},{66,2},{3,67},{67,3},{4,68},{68... | collective-permute-start | bytes 6291464 | tf_op jit(solution)/shard_map/ppermute | solution.py:496
  88.0 84.1 %copy-start.1 = (bf16[1,128,1024]{2,1,0:T(8,128)(2,1)S(1)}, bf16[1,128,1024]{2,1,0:T(8,128)(2,1)}, u32[]{:S(2)}) copy-start(bf16[1,128,1024]{2,1,0:T(8,128)(2,1)} %param.19) | copy-start | bytes 786436
  88.0 84.1 %copy-start.2 = (bf16[512,1024]{1,0:T(8,128)(2,1)S(1)}, bf16[512,1024]{1,0:T(8,128)(2,1)}, u32[]{:S(2)}) copy-start(bf16[512,1024]{1,0:T(8,128)(2,1)} %out_proj_ref.1) | copy-start | bytes 3145732
  88.1 84.1 %copy-start.3 = (bf16[1,128,1024]{2,1,0:T(8,128)(2,1)S(1)}, bf16[1,128,1024]{2,1,0:T(8,128)(2,1)}, u32[]{:S(2)}) copy-start(bf16[1,128,1024]{2,1,0:T(8,128)(2,1)} %param.13) | copy-start | bytes 786436
  88.1 84.1 %copy-start.4 = (f32[1024]{0:T(1024)S(1)}, f32[1024]{0:T(1024)}, u32[]{:S(2)}) copy-start(f32[1024]{0:T(1024)} %param.18) | copy-start | bytes 12292
  172.2 9.6 %copy-start.6 = (bf16[31,1024]{1,0:T(8,128)(2,1)S(1)}, bf16[31,1024]{1,0:T(8,128)(2,1)}, u32[]{:S(2)}) copy-start(bf16[31,1024]{1,0:T(8,128)(2,1)} %param.17) | copy-start | bytes 190468
  172.2 14.6 %copy-start = (bf16[1024,1024]{1,0:T(8,128)(2,1)S(1)}, bf16[1024,1024]{1,0:T(8,128)(2,1)}, u32[]{:S(2)}) copy-start(bf16[1024,1024]{1,0:T(8,128)(2,1)} %conv_out_ref.1) | copy-start | bytes 6291460
  176.9 6.0 %collective-permute-start.2 = (bf16[48,1024]{1,0:T(8,128)(2,1)S(1)}, bf16[48,1024]{1,0:T(8,128)(2,1)S(1)}, u32[]{:S(2)}, u32[]{:S(2)}) collective-permute-start(bf16[48,1024]{1,0:T(8,128)(2,1)S(1)} %get-tuple-element.16), channel_id=1, source_target_pairs={{0,1},{1,2},{2,3},{3,4},{4,5},{5,6},{6,7},{7,8},{8,9},{9,10},{10,1... | collective-permute-start | bytes 294920 | tf_op jit(solution)/shard_map/ppermute | solution.py:503
  180.3 6.5 %collective-permute-start.3 = (bf16[48,1024]{1,0:T(8,128)(2,1)S(1)}, bf16[48,1024]{1,0:T(8,128)(2,1)S(1)}, u32[]{:S(2)}, u32[]{:S(2)}) collective-permute-start(bf16[48,1024]{1,0:T(8,128)(2,1)S(1)} %get-tuple-element.17), channel_id=1, source_target_pairs={{1,0},{2,1},{3,2},{4,3},{5,4},{6,5},{7,6},{8,7},{9,8},{10,9},{11,1... | collective-permute-start | bytes 294920 | tf_op jit(solution)/shard_map/ppermute | solution.py:504
